TPU v7x, 512 devices: a whole 4x4x16 slice. The times are simulated.
512 devices in a mesh: grp: 2 (over y_hi), az: 16 (over x, y_lo, core), ax: 16 (over z).
Axes of the slice: x: 4, y: 4 (y_hi: 2, y_lo: 2; y = y_hi * 2 + y_lo), z: 16, core: 2. Of those that a mesh axis runs over, the one named last changes fastest.
Arguments:
- populations: float32 [2, 27, 2, 512, 2048], P('grp', None, None, 'az', 'ax'), may hold values from 0.4 to 1.6
- relax_rates: float32 [2, 27], replicated, may hold values from 1 to 1.7
- tile_offsets: int32 [16, 16], P('ax'), may hold values from 0 to 15, each once within a row
Outputs:
- populations_next: float32 [2, 27, 2, 512, 2048], P('grp', None, None, 'az', 'ax')
Inputs may be any that keep to these rules, and one draw needn't show every extreme that they name: `tile_offsets`: each row is a permutation of the 16 block offsets.
All inputs are finite; a program needn't handle non-finite values.
Results may differ from a plain program's by a relative error of at most 0.0003.
Values sent between devices are 32-bit elements; how exact they have to be, the bound alone decides.
No kernel may reach another device: no remote copies, remote signals or barrier semaphores. Data moves between devices by JAX's collectives and lax.ppermute only.
A program may use at most 64 MiB of HBM per device.

v0:
```python
import jax
import jax.numpy as jnp
from jax import lax
from jax.sharding import PartitionSpec as P

exact_mode = lax.Precision.HIGHEST


def padded_2(x, sides, width):
    for axis, dim in sides:
        size, length = (lax.axis_size(axis), x.shape[dim])
        up = [(i, (i + 1) % size) for i in range(size)]
        down = [(j, i) for i, j in up]
        last = lax.slice_in_dim(x, length - width, length, axis=dim)
        first = lax.slice_in_dim(x, 0, width, axis=dim)
        before = lax.ppermute(last, axis, up)
        after = lax.ppermute(first, axis, down)
        x = jnp.concatenate([before, x, after], axis=dim)
    return x


def swapped(x, axis, distance):
    return lax.ppermute(x, axis, [(i, i ^ 1 << distance) for i in range(lax.axis_size(axis))])


def single_weight(value):
    return 2.0 / 3.0 if value == 0 else 1.0 / 6.0


def lattice_tables():
    speeds = [
        (radial, beside_all, along)
        for radial in (-1, 0, 1)
        for beside_all in (-1, 0, 1)
        for along in (-1, 0, 1)
    ]
    weights = [
        single_weight(vector[0]) * single_weight(vector[1]) * single_weight(vector[2])
        for vector in speeds
    ]
    powers = [
        (first, second, third) for first in range(3) for second in range(3) for third in range(3)
    ]
    moments = [
        [
            float(vector[0] ** power[0] * vector[1] ** power[1] * vector[2] ** power[2])
            for vector in speeds
        ]
        for power in powers
    ]
    inverse_one = {-1: (0.0, -0.5, 0.5), 0: (1.0, 0.0, -1.0), 1: (0.0, 0.5, 0.5)}
    inverse = [
        [
            inverse_one[vector[0]][power[0]]
            * inverse_one[vector[1]][power[1]]
            * inverse_one[vector[2]][power[2]]
            for power in powers
        ]
        for vector in speeds
    ]
    return (speeds, weights, moments, inverse)


def operators(relax_rates):
    speeds, weights, moments, inverse = lattice_tables()
    keeping = [0.0 if index in (0, 1, 3, 9) else 1.0 for index in range(27)]
    left_table = jnp.asarray(
        [[inverse[row][col] / weights[row] for col in range(27)] for row in range(27)],
        dtype=jnp.float32,
    )
    right_table = jnp.asarray(
        [[moments[row][col] * weights[col] for col in range(27)] for row in range(27)],
        dtype=jnp.float32,
    )
    scaled = relax_rates * jnp.asarray(keeping, dtype=jnp.float32)
    return jnp.einsum("im,gm,mj->gij", left_table, scaled, right_table, precision=exact_mode)


def equilibrium(state):
    speeds, weights, moments, inverse = lattice_tables()
    weight_table = jnp.asarray(weights, dtype=jnp.float32)
    drift_table = jnp.asarray(
        [[float(speeds[row][col]) * weights[row] for col in range(3)] for row in range(27)],
        dtype=jnp.float32,
    )
    speed_table = jnp.asarray(
        [[float(speeds[row][col]) for col in range(3)] for row in range(27)], dtype=jnp.float32
    )
    density = jnp.einsum("i,i...->...", weight_table, state, precision=exact_mode)
    flow = jnp.einsum("ik,i...->k...", drift_table, state, precision=exact_mode) / density
    project = jnp.einsum("ik,k...->i...", speed_table, flow, precision=exact_mode)
    square = jnp.sum(flow * flow, axis=0)
    return density * (1.0 + 3.0 * project + 4.5 * project * project - 1.5 * square)


def relax(state, collision_matrix):
    return state - jnp.einsum(
        "ij,j...->i...", collision_matrix, state - equilibrium(state), precision=exact_mode
    )


def stream(padded, low_ghost, high_ghost, beside_all, axial):
    outgoing = []
    for index in range(27):
        radial_step = index // 9 - 1
        around_step = index // 3 % 3 - 1
        along_step = index % 3 - 1
        moved = padded[
            index,
            :,
            1 - around_step : 1 - around_step + beside_all,
            1 - along_step : 1 - along_step + axial,
        ]
        if radial_step == 1:
            moved = jnp.concatenate([low_ghost[index - 18][None], moved[:-1]], axis=0)
        elif radial_step == -1:
            moved = jnp.concatenate([moved[1:], high_ghost[index][None]], axis=0)
        outgoing.append(moved)
    return jnp.stack(outgoing)


def bounced(post):
    return jnp.stack([post[26 - index, -1] for index in range(9)])


def mirrored(padded, beside_all, axial):
    rows = []
    for index in range(18, 27):
        around_step = index // 3 % 3 - 1
        along_step = index % 3 - 1
        rows.append(
            padded[
                index - 18,
                0,
                1 - around_step : 1 - around_step + beside_all,
                1 - along_step : 1 - along_step + axial,
            ]
        )
    return jnp.stack(rows)


def local(populations, relax_rates, tile_offsets):
    state = populations[0]
    group = lax.axis_index("grp")
    place = lax.axis_index("az")
    count = lax.axis_size("az")
    beside_all = state.shape[2]
    axial = state.shape[3]
    slots = beside_all // count
    annulus = group == 0
    matrices = operators(relax_rates)
    own_matrix = matrices[group]
    fine_matrix = matrices[0]
    rate_fine = relax_rates[0, 12]
    rate_core = relax_rates[1, 12]

    def own_collision(block):
        return relax(block, own_matrix)

    def second_collision(block):
        return relax(block, fine_matrix)

    def advance(block, collide):
        post = collide(block)
        padded = padded_2(post, (("az", 2), ("ax", 3)), 1)
        return (post, padded)

    post_first, padded_first = advance(state, own_collision)
    face_rows = jnp.where(annulus, post_first[:, 0], post_first[:, -1])
    face_balance = equilibrium(face_rows)
    to_core = face_balance[0:9] + 2.0 * rate_fine / rate_core * (face_rows[0:9] - face_balance[0:9])
    to_annulus = face_balance[18:27] + rate_core / (2.0 * rate_fine) * (
        face_rows[18:27] - face_balance[18:27]
    )
    outward = jnp.where(annulus, to_core, to_annulus).reshape(9, count, slots, axial)
    direction = 1 - 2 * group
    partner = jnp.remainder(place + direction * tile_offsets[0], count)
    selector = (jnp.arange(count, dtype=jnp.int32)[:, None] == partner[None, :]).astype(jnp.float32)
    outbound = jnp.einsum("dg,igsx->disx", selector, outward, precision=exact_mode)
    crossed = swapped(outbound, "grp", 0)
    received = lax.all_to_all(crossed, "az", split_axis=0, concat_axis=0, tiled=True)
    inward = jnp.einsum("qg,qisx->igsx", selector, received, precision=exact_mode).reshape(
        9, beside_all, axial
    )
    low_first = jnp.where(annulus, inward, mirrored(padded_first, beside_all, axial))
    high_first = jnp.where(annulus, bounced(post_first), inward)
    middle = stream(padded_first, low_first, high_first, beside_all, axial)
    post_second, padded_second = advance(middle, second_collision)
    finished = stream(padded_second, inward, bounced(post_second), beside_all, axial)
    return jnp.where(annulus, finished, middle)[None]


def solution(mesh):
    in_specs = (P("grp", None, None, "az", "ax"), P(), P("ax", None))
    out_specs = P("grp", None, None, "az", "ax")
    return jax.shard_map(local, mesh=mesh, in_specs=in_specs, out_specs=out_specs, check_vma=False)
```

profile of v0, /device:TPU:1, one launch (start us, length us, event | category | flops | bytes accessed | tf_op | source)
XLA Modules:
  0.0 95.9 jit_solution(5534416426269501158)
XLA Ops:
  0.0 2.3 %fusion.5 = f32[1,2,32,128]{3,0,2,1:T(1,128)S(1)} fusion(f32[27,1,1,1]{0,1,3,2:T(1,128)} %constant.70, f32[27,2,32,128]{3,2,1,0:T(8,128)} %bitcast.478), kind=kOutput, calls=%fused_computation.13 | convolution fusion | flops 2654208 | bytes 917612 | tf_op jit(solution)/shard_map/i,i...->.../dot_general | solution.py:89
  2.3 2.4 %multiply_reduce_fusion.1 = (f32[2,32,128]{2,1,0:T(8,128)S(1)}, f32[3,2,32,128]{3,0,2,1:T(4,128)S(1)}) fusion(f32[2,32,128]{2,1,0:T(8,128)S(1)} %bitcast.482, f32[27,3,1,1]{0,1,3,2:T(4,128)S(1)} %copy-done.21, f32[27,2,32,128]{3,2,1,0:T(8,128)} %bitcast.479), kind=kOutput, calls=%fused_computation.153 | convolution fusion | flops 8028160 | bytes 1048900 | tf_op jit(solution)/shard_map/ik,i...->k.../dot_general | solution.py:90
  4.8 1.1 %fusion.68 = f32[27,2,32,128]{3,0,2,1:T(8,128)S(1)} fusion(f32[27,3,1,1]{0,1,3,2:T(4,128)S(1)} %copy-done.20, f32[3,2,32,128]{3,0,2,1:T(4,128)S(1)} %get-tuple-element.127), kind=kOutput, calls=%fused_computation.319 | convolution fusion | flops 7962624 | bytes 983364 | tf_op jit(solution)/shard_map/ik,k...->i.../dot_general | solution.py:91
  7.3 1.5 %fusion.10 = f32[27,2,32,128]{3,0,2,1:T(8,128)S(1)} fusion(f32[27,2,32,128]{3,2,1,0:T(8,128)S(1)} %fusion.15, f32[2,27,27]{2,1,0:T(8,128)S(1)} %fusion.37, s32[]{:T(128)S(6)} %select_n.54), kind=kOutput, calls=%fused_computation.18 | convolution fusion | flops 71663616 | bytes 1785860 | tf_op jit(solution)/shard_map/ij,j...->i.../dot_general | solution.py:97
  9.4 4.6 %collective-permute-start = (f32[27,2,1,128]{3,2,1,0:T(1,128)S(1)}, f32[27,2,1,128]{3,2,1,0:T(1,128)S(1)}, u32[]{:S(2)}, u32[]{:S(2)}) collective-permute-start(f32[27,2,1,128]{3,2,1,0:T(1,128)S(1)} %get-tuple-element.93), channel_id=1, source_target_pairs={{0,16},{16,32},{32,48},{48,64},{64,80},{80,96},{96,112},{112,128},... | collective-permute-start | bytes 82952 | tf_op jit(solution)/shard_map/ppermute | solution.py:16
  14.0 6.1 %collective-permute-start.1 = (f32[27,2,1,128]{3,2,1,0:T(1,128)S(1)}, f32[27,2,1,128]{3,2,1,0:T(1,128)S(1)}, u32[]{:S(2)}, u32[]{:S(2)}) collective-permute-start(f32[27,2,1,128]{3,2,1,0:T(1,128)S(1)} %get-tuple-element.94), channel_id=1, source_target_pairs={{16,0},{32,16},{48,32},{64,48},{80,64},{96,80},{112,96},{128,112},... | collective-permute-start | bytes 82952 | tf_op jit(solution)/shard_map/ppermute | solution.py:17
  26.1 1.9 %collective-permute-start.3 = (f32[16,9,2,128]{3,0,2,1:T(8,128)S(1)}, f32[16,9,2,128]{3,0,2,1:T(8,128)}, u32[]{:S(2)}, u32[]{:S(2)}) collective-permute-start(f32[16,9,2,128]{3,0,2,1:T(8,128)S(1)} %fusion.35), channel_id=1, source_target_pairs={{0,256},{256,0},{1,257},{257,1},{2,258},{258,2},{3,259},{259,3},{4... | collective-permute-start | bytes 442376 | tf_op jit(solution)/shard_map/ppermute | solution.py:23
  29.5 9.6 %collective-permute-start.2 = (f32[27,2,34,1]{2,1,3,0:T(2,128)S(1)}, f32[27,2,34,1]{2,1,3,0:T(2,128)S(1)}, u32[]{:S(2)}, u32[]{:S(2)}) collective-permute-start(f32[27,2,34,1]{2,1,3,0:T(2,128)S(1)} %copy.119), channel_id=1, source_target_pairs={{1,0},{2,1},{3,2},{4,3},{5,4},{6,5},{7,6},{8,7},{9,8},{10,9},{11,1... | collective-permute-start | bytes 22040 | tf_op jit(solution)/shard_map/ppermute | solution.py:17
  39.1 1.9 %collective-permute-start.4 = (f32[27,2,34,1]{2,1,3,0:T(2,128)S(1)}, f32[27,2,34,1]{2,1,3,0:T(2,128)S(1)}, u32[]{:S(2)}, u32[]{:S(2)}) collective-permute-start(f32[27,2,34,1]{2,1,3,0:T(2,128)S(1)} %copy.132), channel_id=1, source_target_pairs={{0,1},{1,2},{2,3},{3,4},{4,5},{5,6},{6,7},{7,8},{8,9},{9,10},{10,1... | collective-permute-start | bytes 22040 | tf_op jit(solution)/shard_map/ppermute | solution.py:16
  41.6 3.3 %collective-permute-done.4 = f32[27,2,34,1]{2,1,3,0:T(2,128)S(1)} collective-permute-done((f32[27,2,34,1]{2,1,3,0:T(2,128)S(1)}, f32[27,2,34,1]{2,1,3,0:T(2,128)S(1)}, u32[]{:S(2)}, u32[]{:S(2)}) %collective-permute-start.4) | collective-permute-done | bytes 7376 | tf_op jit(solution)/shard_map/ppermute | solution.py:16
  48.4 1.6 %copy.129 = f32[16,9,2,128]{3,2,1,0:T(2,128)} copy(f32[16,9,2,128]{3,0,2,1:T(8,128)} %collective-permute-done.3) | data formatting | bytes 294912 | tf_op jit(solution)/shard_map/ppermute | solution.py:23
  50.0 8.0 %all-to-all-start = ((f32[16,9,2,128]{3,2,1,0:T(2,128)}), f32[16,9,2,128]{3,2,1,0:T(2,128)S(1)}, u32[]{:S(2)}, u32[]{:S(2)}) async-start(f32[16,9,2,128]{3,2,1,0:T(2,128)} %copy.129), calls=%async_computation | async-start | bytes 294912 | tf_op jit(solution)/shard_map/all_to_all | solution.py:181
  59.3 5.0 %all-to-all-done = f32[16,9,2,128]{3,2,1,0:T(2,128)S(1)} async-done(((f32[16,9,2,128]{3,2,1,0:T(2,128)}), f32[16,9,2,128]{3,2,1,0:T(2,128)S(1)}, u32[]{:S(2)}, u32[]{:S(2)}) %all-to-all-start) | async-done | bytes 147488 | tf_op jit(solution)/shard_map/all_to_all | solution.py:181
  68.3 1.2 %fusion.2 = f32[1,2,32,128]{3,0,2,1:T(1,128)S(1)} fusion(f32[27,1,1,1]{0,1,3,2:T(1,128)S(1)} %copy-done.26, f32[27,2,32,128]{3,2,1,0:T(8,128)S(1)} %constant_dynamic-update-slice_fusion.18), kind=kOutput, calls=%fused_computation.10 | convolution fusion | flops 2654208 | bytes 917612 | tf_op jit(solution)/shard_map/i,i...->.../dot_general | solution.py:89
  69.5 1.3 %multiply_reduce_fusion = (f32[2,32,128]{2,1,0:T(8,128)S(1)}, f32[3,2,32,128]{3,0,2,1:T(4,128)S(1)}) fusion(f32[2,32,128]{2,1,0:T(8,128)S(1)} %bitcast.484, f32[27,3,1,1]{0,1,3,2:T(4,128)S(1)} %copy-done.21, f32[27,2,32,128]{3,2,1,0:T(8,128)S(1)} %constant_dynamic-update-slice_fusion.18), kind=kOutput, calls=%fused_computation.152 | convolution fusion | flops 8028160 | bytes 1048900 | tf_op jit(solution)/shard_map/ik,i...->k.../dot_general | solution.py:90
  70.8 1.1 %fusion.70 = f32[27,2,32,128]{3,0,2,1:T(8,128)S(1)} fusion(f32[27,3,1,1]{0,1,3,2:T(4,128)S(1)} %copy-done.20, f32[3,2,32,128]{3,0,2,1:T(4,128)S(1)} %get-tuple-element.131), kind=kOutput, calls=%fused_computation.321 | convolution fusion | flops 7962624 | bytes 983364 | tf_op jit(solution)/shard_map/ik,k...->i.../dot_general | solution.py:91
  72.6 1.5 %fusion.8 = f32[27,2,32,128]{3,0,2,1:T(8,128)S(1)} fusion(f32[27,2,32,128]{3,2,1,0:T(8,128)S(1)} %fusion.19, f32[2,27,27]{2,1,0:T(8,128)S(1)} %copy-done.17), kind=kOutput, calls=%fused_computation.16 | convolution fusion | flops 71663616 | bytes 1785856 | tf_op jit(solution)/shard_map/ij,j...->i.../dot_general | solution.py:97
  74.7 2.6 %collective-permute-start.5 = (f32[27,2,1,128]{3,2,1,0:T(1,128)S(1)}, f32[27,2,1,128]{3,2,1,0:T(1,128)S(1)}, u32[]{:S(2)}, u32[]{:S(2)}) collective-permute-start(f32[27,2,1,128]{3,2,1,0:T(1,128)S(1)} %get-tuple-element.71), channel_id=1, source_target_pairs={{0,16},{16,32},{32,48},{48,64},{64,80},{80,96},{96,112},{112,128},... | collective-permute-start | bytes 82952 | tf_op jit(solution)/shard_map/ppermute | solution.py:16
  77.3 1.9 %collective-permute-start.6 = (f32[27,2,1,128]{3,2,1,0:T(1,128)S(1)}, f32[27,2,1,128]{3,2,1,0:T(1,128)S(1)}, u32[]{:S(2)}, u32[]{:S(2)}) collective-permute-start(f32[27,2,1,128]{3,2,1,0:T(1,128)S(1)} %get-tuple-element.72), channel_id=1, source_target_pairs={{16,0},{32,16},{48,32},{64,48},{80,64},{96,80},{112,96},{128,112},... | collective-permute-start | bytes 82952 | tf_op jit(solution)/shard_map/ppermute | solution.py:17
  80.2 2.3 %collective-permute-done.6 = f32[27,2,1,128]{3,2,1,0:T(1,128)S(1)} collective-permute-done((f32[27,2,1,128]{3,2,1,0:T(1,128)S(1)}, f32[27,2,1,128]{3,2,1,0:T(1,128)S(1)}, u32[]{:S(2)}, u32[]{:S(2)}) %collective-permute-start.6) | collective-permute-done | bytes 27680 | tf_op jit(solution)/shard_map/ppermute | solution.py:17
  83.9 1.9 %collective-permute-start.7 = (f32[27,2,34,1]{2,1,3,0:T(2,128)S(1)}, f32[27,2,34,1]{2,1,3,0:T(2,128)S(1)}, u32[]{:S(2)}, u32[]{:S(2)}) collective-permute-start(f32[27,2,34,1]{2,1,3,0:T(2,128)S(1)} %copy.140), channel_id=1, source_target_pairs={{1,0},{2,1},{3,2},{4,3},{5,4},{6,5},{7,6},{8,7},{9,8},{10,9},{11,1... | collective-permute-start | bytes 22040 | tf_op jit(solution)/shard_map/ppermute | solution.py:17
  85.9 3.4 %collective-permute-start.8 = (f32[27,2,34,1]{2,1,3,0:T(2,128)S(1)}, f32[27,2,34,1]{2,1,3,0:T(2,128)S(1)}, u32[]{:S(2)}, u32[]{:S(2)}) collective-permute-start(f32[27,2,34,1]{2,1,3,0:T(2,128)S(1)} %copy.142), channel_id=1, source_target_pairs={{0,1},{1,2},{2,3},{3,4},{4,5},{5,6},{6,7},{7,8},{8,9},{9,10},{10,1... | collective-permute-start | bytes 22040 | tf_op jit(solution)/shard_map/ppermute | solution.py:16
  89.3 2.4 %collective-permute-done.8 = f32[27,2,34,1]{2,1,3,0:T(2,128)S(1)} collective-permute-done((f32[27,2,34,1]{2,1,3,0:T(2,128)S(1)}, f32[27,2,34,1]{2,1,3,0:T(2,128)S(1)}, u32[]{:S(2)}, u32[]{:S(2)}) %collective-permute-start.8) | collective-permute-done | bytes 7376 | tf_op jit(solution)/shard_map/ppermute | solution.py:16
  94.8 1.1 %broadcast_select_fusion = f32[1,27,2,32,128]{4,3,2,1,0:T(8,128)} fusion(f32[1,27,2,32,128]{4,3,2,1,0:T(8,128)S(1)} %constant_dynamic-update-slice_fusion.45, f32[1,27,2,32,128]{4,3,2,1,0:T(8,128)S(1)} %copy-done.2, pred[]{:T(512)S(6)} %eq.20), kind=kLoop, calls=%fused_computation.40 | loop fusion | flops 221184 | bytes 2654209 | tf_op jit(solution)/shard_map/jit(_where)/select_n | solution.py:190
  (211 shorter events, 22.7 us)
Async XLA Ops:
  0.0 2.3 %copy-start.21 = (f32[27,3,1,1]{0,1,3,2:T(4,128)S(1)}, f32[27,3,1,1]{0,1,3,2:T(4,128)}, u32[]{:S(2)}) copy-start(f32[27,3,1,1]{0,1,3,2:T(4,128)} %constant.72) | copy-start | bytes 976
  0.0 4.7 %copy-start.23 = (f32[2,27]{1,0:T(2,128)S(1)}, f32[2,27]{1,0:T(2,128)}, u32[]{:S(2)}) copy-start(f32[2,27]{1,0:T(2,128)} %param.16) | copy-start | bytes 652
  0.0 4.7 %copy-start.28 = (f32[27]{0:T(128)S(1)}, f32[27]{0:T(128)}, u32[]{:S(2)}) copy-start(f32[27]{0:T(128)} %constant.62.clone) | copy-start | bytes 328
  0.0 4.7 %copy-start.20 = (f32[27,3,1,1]{0,1,3,2:T(4,128)S(1)}, f32[27,3,1,1]{0,1,3,2:T(4,128)}, u32[]{:S(2)}) copy-start(f32[27,3,1,1]{0,1,3,2:T(4,128)} %constant.71) | copy-start | bytes 976
  2.3 3.5 %copy-start = (f32[1,27,2,32,128]{4,3,2,1,0:T(8,128)S(1)}, f32[1,27,2,32,128]{4,3,2,1,0:T(8,128)}, u32[]{:S(2)}) copy-start(f32[1,27,2,32,128]{4,3,2,1,0:T(8,128)} %param.15) | copy-start | bytes 2654212
  9.4 18.5 %collective-permute-start = (f32[27,2,1,128]{3,2,1,0:T(1,128)S(1)}, f32[27,2,1,128]{3,2,1,0:T(1,128)S(1)}, u32[]{:S(2)}, u32[]{:S(2)}) collective-permute-start(f32[27,2,1,128]{3,2,1,0:T(1,128)S(1)} %get-tuple-element.93), channel_id=1, source_target_pairs={{0,16},{16,32},{32,48},{48,64},{64,80},{80,96},{96,112},{112,128},... | collective-permute-start | bytes 82952 | tf_op jit(solution)/shard_map/ppermute | solution.py:16
  14.0 14.0 %collective-permute-start.1 = (f32[27,2,1,128]{3,2,1,0:T(1,128)S(1)}, f32[27,2,1,128]{3,2,1,0:T(1,128)S(1)}, u32[]{:S(2)}, u32[]{:S(2)}) collective-permute-start(f32[27,2,1,128]{3,2,1,0:T(1,128)S(1)} %get-tuple-element.94), channel_id=1, source_target_pairs={{16,0},{32,16},{48,32},{64,48},{80,64},{96,80},{112,96},{128,112},... | collective-permute-start | bytes 82952 | tf_op jit(solution)/shard_map/ppermute | solution.py:17
  22.6 1.3 %copy-start.25 = (f32[27,3,1]{0,1,2:T(4,128)S(1)}, f32[27,3,1]{0,1,2:T(4,128)}, u32[]{:S(2)}) copy-start(f32[27,3,1]{0,1,2:T(4,128)} %constant.75) | copy-start | bytes 976
  22.6 2.0 %copy-start.24 = (f32[27,3,1]{0,1,2:T(4,128)S(1)}, f32[27,3,1]{0,1,2:T(4,128)}, u32[]{:S(2)}) copy-start(f32[27,3,1]{0,1,2:T(4,128)} %constant.74) | copy-start | bytes 976
  23.9 1.7 %copy-start.29 = (s32[1,16]{1,0:T(1,128)S(1)}, s32[1,16]{1,0:T(1,128)}, u32[]{:S(2)}) copy-start(s32[1,16]{1,0:T(1,128)} %param.17) | copy-start | bytes 196
  25.6 2.9 %copy-start.22 = (s32[16]{0:T(128)}, s32[16]{0:T(128)S(1)}, u32[]{:S(2)}) copy-start(s32[16]{0:T(128)S(1)} %fusion.57) | copy-start | bytes 196
  26.1 22.3 %collective-permute-start.3 = (f32[16,9,2,128]{3,0,2,1:T(8,128)S(1)}, f32[16,9,2,128]{3,0,2,1:T(8,128)}, u32[]{:S(2)}, u32[]{:S(2)}) collective-permute-start(f32[16,9,2,128]{3,0,2,1:T(8,128)S(1)} %fusion.35), channel_id=1, source_target_pairs={{0,256},{256,0},{1,257},{257,1},{2,258},{258,2},{3,259},{259,3},{4... | collective-permute-start | bytes 442376 | tf_op jit(solution)/shard_map/ppermute | solution.py:23
  29.5 15.9 %collective-permute-start.2 = (f32[27,2,34,1]{2,1,3,0:T(2,128)S(1)}, f32[27,2,34,1]{2,1,3,0:T(2,128)S(1)}, u32[]{:S(2)}, u32[]{:S(2)}) collective-permute-start(f32[27,2,34,1]{2,1,3,0:T(2,128)S(1)} %copy.119), channel_id=1, source_target_pairs={{1,0},{2,1},{3,2},{4,3},{5,4},{6,5},{7,6},{8,7},{9,8},{10,9},{11,1... | collective-permute-start | bytes 22040 | tf_op jit(solution)/shard_map/ppermute | solution.py:17
  39.1 5.8 %collective-permute-start.4 = (f32[27,2,34,1]{2,1,3,0:T(2,128)S(1)}, f32[27,2,34,1]{2,1,3,0:T(2,128)S(1)}, u32[]{:S(2)}, u32[]{:S(2)}) collective-permute-start(f32[27,2,34,1]{2,1,3,0:T(2,128)S(1)} %copy.132), channel_id=1, source_target_pairs={{0,1},{1,2},{2,3},{3,4},{4,5},{5,6},{6,7},{7,8},{8,9},{9,10},{10,1... | collective-permute-start | bytes 22040 | tf_op jit(solution)/shard_map/ppermute | solution.py:16
  50.0 14.3 %all-to-all-start = ((f32[16,9,2,128]{3,2,1,0:T(2,128)}), f32[16,9,2,128]{3,2,1,0:T(2,128)S(1)}, u32[]{:S(2)}, u32[]{:S(2)}) async-start(f32[16,9,2,128]{3,2,1,0:T(2,128)} %copy.129), calls=%async_computation | async-start | bytes 294912 | tf_op jit(solution)/shard_map/all_to_all | solution.py:181
  64.3 2.1 %copy-start.15 = (f32[1,32,128]{2,1,0:T(8,128)S(1)}, f32[1,32,128]{2,1,0:T(8,128)}, u32[]{:S(2)}) copy-start(f32[1,32,128]{2,1,0:T(8,128)} %get-tuple-element.51) | copy-start | bytes 49156
  64.3 2.1 %copy-start.7 = (f32[1,32,128]{2,1,0:T(8,128)S(1)}, f32[1,32,128]{2,1,0:T(8,128)}, u32[]{:S(2)}) copy-start(f32[1,32,128]{2,1,0:T(8,128)} %maximum_bitcast_fusion.56) | copy-start | bytes 49156
  65.2 1.2 %copy-start.13 = (f32[1,32,128]{2,1,0:T(8,128)S(1)}, f32[1,32,128]{2,1,0:T(8,128)}, u32[]{:S(2)}) copy-start(f32[1,32,128]{2,1,0:T(8,128)} %get-tuple-element.52) | copy-start | bytes 49156
  65.2 1.3 %copy-start.11 = (f32[1,32,128]{2,1,0:T(8,128)S(1)}, f32[1,32,128]{2,1,0:T(8,128)}, u32[]{:S(2)}) copy-start(f32[1,32,128]{2,1,0:T(8,128)} %get-tuple-element.73) | copy-start | bytes 49156
  65.2 1.3 %copy-start.12 = (f32[1,32,128]{2,1,0:T(8,128)S(1)}, f32[1,32,128]{2,1,0:T(8,128)}, u32[]{:S(2)}) copy-start(f32[1,32,128]{2,1,0:T(8,128)} %get-tuple-element.41) | copy-start | bytes 49156
  74.7 4.7 %collective-permute-start.5 = (f32[27,2,1,128]{3,2,1,0:T(1,128)S(1)}, f32[27,2,1,128]{3,2,1,0:T(1,128)S(1)}, u32[]{:S(2)}, u32[]{:S(2)}) collective-permute-start(f32[27,2,1,128]{3,2,1,0:T(1,128)S(1)} %get-tuple-element.71), channel_id=1, source_target_pairs={{0,16},{16,32},{32,48},{48,64},{64,80},{80,96},{96,112},{112,128},... | collective-permute-start | bytes 82952 | tf_op jit(solution)/shard_map/ppermute | solution.py:16
  77.3 5.2 %collective-permute-start.6 = (f32[27,2,1,128]{3,2,1,0:T(1,128)S(1)}, f32[27,2,1,128]{3,2,1,0:T(1,128)S(1)}, u32[]{:S(2)}, u32[]{:S(2)}) collective-permute-start(f32[27,2,1,128]{3,2,1,0:T(1,128)S(1)} %get-tuple-element.72), channel_id=1, source_target_pairs={{16,0},{32,16},{48,32},{64,48},{80,64},{96,80},{112,96},{128,112},... | collective-permute-start | bytes 82952 | tf_op jit(solution)/shard_map/ppermute | solution.py:17
  83.9 8.3 %collective-permute-start.7 = (f32[27,2,34,1]{2,1,3,0:T(2,128)S(1)}, f32[27,2,34,1]{2,1,3,0:T(2,128)S(1)}, u32[]{:S(2)}, u32[]{:S(2)}) collective-permute-start(f32[27,2,34,1]{2,1,3,0:T(2,128)S(1)} %copy.140), channel_id=1, source_target_pairs={{1,0},{2,1},{3,2},{4,3},{5,4},{6,5},{7,6},{8,7},{9,8},{10,9},{11,1... | collective-permute-start | bytes 22040 | tf_op jit(solution)/shard_map/ppermute | solution.py:17
  85.9 5.8 %collective-permute-start.8 = (f32[27,2,34,1]{2,1,3,0:T(2,128)S(1)}, f32[27,2,34,1]{2,1,3,0:T(2,128)S(1)}, u32[]{:S(2)}, u32[]{:S(2)}) collective-permute-start(f32[27,2,34,1]{2,1,3,0:T(2,128)S(1)} %copy.142), channel_id=1, source_target_pairs={{0,1},{1,2},{2,3},{3,4},{4,5},{5,6},{6,7},{7,8},{8,9},{9,10},{10,1... | collective-permute-start | bytes 22040 | tf_op jit(solution)/shard_map/ppermute | solution.py:16
  (16 other events, 14.2 us)
where the time goes:
time: 97.8 us; the launch traced here: 95.9 us
  starting transfers between devices  41.8 us (43%)
  matrix products  15.7 us (16%)
  waiting for transfers between devices  13.1 us (13%)
  local copies, waits for them, and re-layouts  11.5 us (12%)
  other arithmetic  10.5 us (11%)
  between operations  3.29 us (3%)
    ppermute x4, starting transfers between devices, padded_2(): after = lax.ppermute(first, axis, down)  19.5 us
    ppermute x4, starting transfers between devices, padded_2(): before = lax.ppermute(last, axis, up)  12.4 us
    all_to_all x1, starting transfers between devices, local(): lax.all_to_all(crossed, 'az', split_axis=0, concat_axis=0, tiled=True)  7.97 us
    ppermute x4, waiting for transfers between devices, padded_2(): before = lax.ppermute(last, axis, up)  5.7 us
    all_to_all x1, waiting for transfers between devices, local(): lax.all_to_all(crossed, 'az', split_axis=0, concat_axis=0, tiled=True)  5.03 us
    unnamed x72, local copies, waits for them, and re-layouts  4.4 us
    dot_general x3, matrix products, equilibrium(): jnp.einsum('ik,i...->k...', drift_table, state, precision=exact_mode)  4.36 us
    dot_general x3, matrix products, equilibrium(): jnp.einsum('i,i...->...', weight_table, state, precision=exact_mode)  4.21 us
  transfers between devices with their start and end apart: 10, of which 4 were waited for; matrix products, arithmetic and copies ran while one was open for 11% of the time, Pallas kernels for 0%

commit v1 on v0

v1 whole, which is shorter than its diff:
```python
import functools

import jax
import jax.numpy as jnp
from jax import lax
from jax.experimental import pallas as pl
from jax.experimental.pallas import tpu as pltpu
from jax.sharding import PartitionSpec as P

RADIAL, ROWS, FRAME, LANES = 2, 32, 40, 128
COUNT, SLOTS = 16, 2
SLOT_ROWS = 48
CORNERS = 45
EDGE = 36
OFFSET_LANE = 108
exact_mode = lax.Precision.HIGHEST
speeds = [(cr, ca, cx) for cr in (-1, 0, 1) for ca in (-1, 0, 1) for cx in (-1, 0, 1)]


def at(cr, ca, cx):
    return 9 * (cr + 1) + 3 * (ca + 1) + (cx + 1)


def moments(g):
    for stride in (1, 3, 9):
        out = [None] * 27
        for base in range(27):
            if base // stride % 3 == 0:
                low, mid, high = g[base], g[base + stride], g[base + 2 * stride]
                even = high + low
                out[base] = even + 4.0 * mid
                out[base + stride] = high - low
                out[base + 2 * stride] = even
        g = out
    return g


def balance_moments(m):
    third, ninth = 1.0 / 3.0, 1.0 / 9.0
    rho, jx, ja, jr = m[0], m[1], m[3], m[9]
    inverse = 1.0 / rho
    ur, ua, ux = jr * inverse, ja * inverse, jx * inverse
    rr, aa, xx = jr * ur, ja * ua, jx * ux
    rho3, rho9 = rho * third, rho * ninth
    jr3, ja3, jx3 = jr * third, ja * third, jx * third
    ra, rx, ax = jr * ua, jr * ux, ja * ux
    e = [None] * 27
    e[12], e[10], e[4] = ra, rx, ax
    e[18], e[6], e[2] = rho3 + rr, rho3 + aa, rho3 + xx
    e[21], e[19], e[15], e[11], e[5], e[7] = ja3, jx3, jr3, jr3, ja3, jx3
    e[22], e[16], e[14] = ax * third, rx * third, ra * third
    e[24], e[20], e[8] = rho9 + (rr + aa) * third, rho9 + (rr + xx) * third, rho9 + (aa + xx) * third
    e[25], e[23], e[17] = jx * ninth, ja * ninth, jr * ninth
    e[26] = rho * (1.0 / 27.0) + (rr + aa + xx) * ninth
    return e


def relax(g, rates):
    m = moments(g)
    e = balance_moments(m)
    d = [None] * 27
    for k in range(27):
        if k not in (0, 1, 3, 9):
            d[k] = (m[k] if e[k] is None else m[k] - e[k]) * (rates[k] * 0.125)
    for stride in (1, 3, 9):
        out = [None] * 27
        for base in range(27):
            if base // stride % 3 == 0:
                low, mid, high = d[base], d[base + stride], d[base + 2 * stride]
                out[base] = high if mid is None else high - mid
                out[base + stride] = -0.5 * high if low is None else 0.5 * (low - high)
                out[base + 2 * stride] = high if mid is None else high + mid
        d = out
    return [g[i] - d[i] for i in range(27)]


def rescaled(g, side, factor):
    m = moments(g)
    rho = m[0] * (1.0 / 216.0)
    inverse = 1.0 / m[0]
    ur, ua, ux = m[9] * inverse, m[3] * inverse, m[1] * inverse
    rest = 1.0 - 1.5 * (ur * ur + ua * ua + ux * ux)
    out = []
    for ca in (-1, 0, 1):
        for cx in (-1, 0, 1):
            along = side * ur
            along = along + ca * ua if ca else along
            along = along + cx * ux if cx else along
            e = rho * (rest + along * (3.0 + 4.5 * along))
            out.append(e + factor * (g[at(side, ca, cx)] - e))
    return out


def halo_entries(annulus, sense):
    out = []
    for depth, ca in ((1, sense), (1, 0), (2, sense)):
        if not annulus and (depth, ca) != (1, sense):
            continue
        for cx in (-1, 0, 1):
            out += [(at(0, ca, cx), 0, depth), (at(0, ca, cx), 1, depth)]
            out += [(at(1, ca, cx), 0, depth), (at(-1, ca, cx), 1, depth)]
    if annulus:
        out += [(at(1, ca, cx), 1, 1) for ca in (-1, 0, 1) for cx in (-1, 0, 1)]
    else:
        out += [(at(-1, sense, cx), 0, 1) for cx in (-1, 0, 1)]
    return out


def lanes_of(rows):
    return lax.broadcasted_iota(jnp.int32, (rows, LANES), 1)


def rows_of(rows, lanes=LANES):
    return lax.broadcasted_iota(jnp.int32, (rows, lanes), 0)


def group_and_place():
    return lax.axis_index("grp"), lax.axis_index("az")


def partner(place, group, offset):
    return (place + (1 - 2 * group) * offset + COUNT) & (COUNT - 1)


def pack_kernel(offsets, pops, low, high):
    lane, row = lanes_of(ROWS), rows_of(ROWS)
    column = jnp.zeros((ROWS, LANES), jnp.float32)
    for q in range(COUNT):
        column = jnp.where(row // SLOTS == q, offsets[0, q].astype(jnp.float32), column)
    column = jnp.where(lane == OFFSET_LANE, column, 0.0)
    first, last = column, column
    for j in range(54):
        tile = pops[j // 2, j % 2]
        own = lane // 2 == j
        first = jnp.where(own, pltpu.roll(tile, 2 * j, 1) if j else tile, first)
        last = jnp.where(own, pltpu.roll(tile, 2 * j + 2, 1), last)
    low[...] = first
    high[...] = last


def collide_kernel(rates, pops, post):
    group, _ = group_and_place()

    def chunk(step, carry):
        r, rows = step // 4, pl.ds(pl.multiple_of(step % 4 * 8, 8), 8)
        g = [pops[i, r, rows, :] for i in range(27)]
        for i, value in enumerate(relax(g, [rates[group, k] for k in range(27)])):
            post[i, r, rows, :] = value
        return carry

    lax.fori_loop(0, 8, chunk, 0)


def fill_kernel(offsets, rates, post, below, above, strips, slots, face):
    group, place = group_and_place()
    lane = lanes_of(ROWS)
    for j in range(54):
        up = pltpu.roll(above[...], (-2 * j) % LANES, 1) if j else above[...]
        down = pltpu.roll(below[...], (126 - 2 * j) % LANES, 1)
        strips[j // 2, j % 2] = jnp.where(lane < 64, up, down)

    def chunk(step, carry):
        r, rows = step // 4, pl.ds(pl.multiple_of(step % 4 * 8, 8), 8)
        g = [strips[i, r, rows, :] for i in range(27)]
        for i, value in enumerate(relax(g, [rates[group, k] for k in range(27)])):
            strips[i, r, rows, :] = value
        return carry

    lax.fori_loop(0, 8, chunk, 0)
    fine, coarse = rates[0, 12], rates[1, 12]

    def faces(source, tile, r, side, factor):
        def chunk(step, carry):
            rows = pl.ds(pl.multiple_of(step * 8, 8), 8)
            g = [source[i, r, rows, :] for i in range(27)]
            for i, value in enumerate(rescaled(g, side, factor)):
                face[i, tile, rows, :] = value
            return carry

        lax.fori_loop(0, 4, chunk, 0)

    other = COUNT * (1 - group)
    own = COUNT * group

    def halos(annulus):
        for sense in (1, -1):
            slot = own + ((place + sense + COUNT) & (COUNT - 1))
            corners = [jnp.zeros((1, LANES), jnp.float32)] * 2
            narrow = lax.broadcasted_iota(jnp.int32, (1, LANES), 1)
            for n, (i, r, depth) in enumerate(halo_entries(annulus, sense)):
                row = ROWS - depth if sense == 1 else depth - 1
                slots[slot, n : n + 1, :] = post[i, r, row : row + 1, :]
                turned = pltpu.roll(strips[i, r, row : row + 1, :], 4 * (n % 32) + 2, 1)
                corners[n // 32] = jnp.where(narrow // 4 == n % 32, turned, corners[n // 32])
            for k in range(2):
                slots[slot, CORNERS + k : CORNERS + k + 1, :] = corners[k]

    @pl.when(group == 0)
    def _():
        halos(True)
        faces(post, 0, 0, -1, 2.0 * fine / coarse)

    @pl.when(group == 1)
    def _():
        halos(False)
        faces(post, 0, 1, 1, coarse / (2.0 * fine))
        faces(strips, 1, 1, 1, coarse / (2.0 * fine))

    for q in range(COUNT):
        slot = other + partner(place, group, offsets[0, q])
        for i in range(9):
            slots[slot, 2 * i : 2 * i + 2, :] = face[i, 0, 2 * q : 2 * q + 2, :]

    @pl.when(group == 1)
    def _():
        after = other + ((place - offsets[0, COUNT - 1] + 1 + COUNT) & (COUNT - 1))
        before = other + ((place - offsets[0, 0] - 1 + COUNT) & (COUNT - 1))
        for i in range(9):
            slots[after, 18 + i : 19 + i, :] = face[i, 0, ROWS - 1 : ROWS, :]
            slots[before, 27 + i : 28 + i, :] = face[i, 0, 0:1, :]
        wide, row = lanes_of(ROWS), rows_of(ROWS)
        kind, receiver = wide // COUNT, wide % COUNT
        shift = jnp.where(kind == 2, 1, jnp.where(kind == 3, -1, 0))
        fits = ((kind < 2) & (row % 2 == kind)) | ((kind == 2) & (row == ROWS - 1)) | ((kind == 3) & (row == 0))
        picks, values = [], []
        for message, first, turn in ((below, 0, 1), (above, 9, 0)):
            offset = jnp.broadcast_to(message[:, OFFSET_LANE : OFFSET_LANE + 1], (ROWS, LANES)).astype(jnp.int32)
            target = (place - offset + shift + 2 * COUNT) & (COUNT - 1)
            picks.append(jnp.where(fits & (receiver == target), 1.0, 0.0))
            packed = jnp.zeros((ROWS, LANES), jnp.float32)
            for i in range(9):
                packed = jnp.where(wide == first + i, pltpu.roll(face[i, 1], first + i + turn, 1) if first + i + turn else face[i, 1], packed)
            values.append(packed)
        sent = lax.dot_general(
            jnp.concatenate(picks, 0),
            jnp.concatenate(values, 0),
            (((0,), (0,)), ((), ())),
            precision=exact_mode,
            preferred_element_type=jnp.float32,
        )
        line = sent[0:COUNT]
        for k in range(1, 4):
            line = line + pltpu.roll(sent[COUNT * k : COUNT * (k + 1)], 32 * k, 1)
        for e in range(COUNT):
            slots[other + e, EDGE : EDGE + 1, :] = line[e : e + 1]


def shifted(main, strip, ca, cx, lane):
    if ca:
        main, strip = pltpu.roll(main, ca % FRAME, 0), pltpu.roll(strip, ca % FRAME, 0)
    if cx:
        turned, around = pltpu.roll(main, cx % LANES, 1), pltpu.roll(strip, cx % LANES, 1)
        edge = lane == (0 if cx == 1 else LANES - 1)
        main, strip = jnp.where(edge, around, turned), jnp.where(edge, turned, around)
    return main, strip


def finish_kernel(offsets, rates, post, strips, slots, below, above, out, halo, ghost, mid):
    group, place = group_and_place()
    other = COUNT * (1 - group)
    own = COUNT * group
    lane = lanes_of(FRAME)

    def halos(annulus):
        for sense in (1, -1):
            slot = own + ((place - sense + COUNT) & (COUNT - 1))
            for n, (i, r, depth) in enumerate(halo_entries(annulus, sense)):
                row = 8 - depth if sense == 1 else depth - 1
                halo[i, r, 0, row : row + 1, :] = slots[slot, n : n + 1, :]
                line = CORNERS + n // 32
                turned = pltpu.roll(slots[slot, line : line + 1, :], (-4 * (n % 32) - 2) % LANES, 1)
                halo[i, r, 1, row : row + 1, :] = turned

    for q in range(COUNT):
        slot = other + partner(place, group, offsets[0, q])
        for i in range(9):
            ghost[i, 0, 2 * q : 2 * q + 2, :] = slots[slot, 2 * i : 2 * i + 2, :]

    def framed(i, r):
        main = jnp.concatenate([post[i, r], halo[i, r, 0]], 0)
        strip = jnp.concatenate([strips[i, r], halo[i, r, 1]], 0)
        return main, strip

    @pl.when(group == 1)
    def _():
        halos(False)
        for i, (cr, ca, cx) in enumerate(speeds):
            for r in range(RADIAL):
                source = (i, r - cr)
                if r - cr == -1:
                    source = (i - 18, 0)
                if r - cr == RADIAL:
                    out[i, r] = ghost[i, 0, 0:ROWS]
                else:
                    out[i, r] = shifted(*framed(*source), ca, cx, lane)[0][0:ROWS]

    @pl.when(group == 0)
    def _():
        halos(True)
        before = other + ((place - 1 + offsets[0, COUNT - 1] + COUNT) & (COUNT - 1))
        after = other + ((place + 1 + offsets[0, 0] + COUNT) & (COUNT - 1))
        for i in range(9):
            ghost[i, 0, FRAME - 1 : FRAME, :] = slots[before, 18 + i : 19 + i, :]
            ghost[i, 0, ROWS : ROWS + 1, :] = slots[after, 27 + i : 28 + i, :]
        received = jnp.concatenate([slots[other + d, EDGE : EDGE + 1, :] for d in range(COUNT)], 0)
        stack = jnp.concatenate([received] + [pltpu.roll(received, LANES - 32 * k, 1) for k in range(1, 4)], 0)
        row, wide = rows_of(FRAME, 64), lax.broadcasted_iota(jnp.int32, (FRAME, 64), 1)
        kind, sender = wide // COUNT, wide % COUNT
        shift = jnp.where(kind == 2, -1, jnp.where(kind == 3, 1, 0))
        fits = ((kind < 2) & (row % 2 == kind) & (row < ROWS)) | ((kind == 2) & (row == FRAME - 1)) | ((kind == 3) & (row == ROWS))
        picked = []
        for message in (below, above):
            offset = jnp.broadcast_to(message[:, OFFSET_LANE : OFFSET_LANE + 1], (ROWS, 64))
            tail = jnp.where(rows_of(8, 64) == 0, offset[0:1], offset[ROWS - 1 : ROWS])
            offset = jnp.concatenate([offset, tail], 0).astype(jnp.int32)
            source = (place + offset + shift + COUNT) & (COUNT - 1)
            pick = jnp.where(fits & (sender == source), 1.0, 0.0)
            picked.append(
                lax.dot_general(
                    pick, stack, (((1,), (0,)), ((), ())), precision=exact_mode, preferred_element_type=jnp.float32
                )
            )
        for i in range(9):
            left = pltpu.roll(picked[0], LANES - 1 - i, 1)
            right = pltpu.roll(picked[1], LANES - 9 - i, 1)
            ghost[i, 1] = jnp.where(lane < 64, right, left)

        for i, (cr, ca, cx) in enumerate(speeds):
            for r in range(RADIAL):
                if r - cr == -1:
                    main, strip = ghost[i - 18, 0], ghost[i - 18, 1]
                elif r - cr == RADIAL:
                    main, strip = framed(26 - i, 1)
                else:
                    main, strip = shifted(*framed(i, r - cr), ca, cx, lane)
                mid[i, r, 0] = main
                mid[i, r, 1] = strip

        def chunk(step, carry):
            r, tile, rows = step // 10, step // 5 % 2, pl.ds(pl.multiple_of(step % 5 * 8, 8), 8)
            g = [mid[i, r, tile, rows, :] for i in range(27)]
            for i, value in enumerate(relax(g, [rates[0, k] for k in range(27)])):
                mid[i, r, tile, rows, :] = value
            return carry

        lax.fori_loop(0, 20, chunk, 0)
        for i, (cr, ca, cx) in enumerate(speeds):
            for r in range(RADIAL):
                if r - cr == -1:
                    out[i, r] = ghost[i - 18, 0, 0:ROWS]
                elif r - cr == RADIAL:
                    out[i, r] = mid[26 - i, 1, 0, 0:ROWS]
                else:
                    main, strip = mid[i, r - cr, 0], mid[i, r - cr, 1]
                    out[i, r] = shifted(main, strip, ca, cx, lane)[0][0:ROWS]


def local(populations, relax_rates, tile_offsets):
    shape = functools.partial(jax.ShapeDtypeStruct, dtype=jnp.float32)
    block = (27, RADIAL, ROWS, LANES)
    params = pltpu.CompilerParams(vmem_limit_bytes=24 << 20)
    smem, vmem = pl.BlockSpec(memory_space=pltpu.SMEM), pl.BlockSpec(memory_space=pltpu.VMEM)
    state = populations[0]
    low, high = pl.pallas_call(
        pack_kernel,
        out_shape=(shape((ROWS, LANES)), shape((ROWS, LANES))),
        in_specs=[smem, vmem],
        out_specs=(vmem, vmem),
        compiler_params=params,
        name="pack",
    )(tile_offsets, state)
    size = lax.axis_size("ax")
    up = [(i, (i + 1) % size) for i in range(size)]
    below = lax.ppermute(high, "ax", up)
    above = lax.ppermute(low, "ax", [(j, i) for i, j in up])
    post = pl.pallas_call(
        collide_kernel,
        out_shape=shape(block),
        in_specs=[smem, vmem],
        out_specs=vmem,
        compiler_params=params,
        cost_estimate=pl.CostEstimate(flops=80_000_000, bytes_accessed=1_800_000, transcendentals=0),
        name="collide",
    )(relax_rates, state)
    strips, slots = pl.pallas_call(
        fill_kernel,
        out_shape=(shape(block), shape((2 * COUNT, SLOT_ROWS, LANES))),
        in_specs=[smem, smem, vmem, vmem, vmem],
        out_specs=(vmem, vmem),
        scratch_shapes=[pltpu.VMEM((9, 2, ROWS, LANES), jnp.float32)],
        compiler_params=params,
        name="fill",
    )(tile_offsets, relax_rates, post, below, above)
    slots = lax.all_to_all(slots, ("grp", "az"), split_axis=0, concat_axis=0, tiled=True)
    out = pl.pallas_call(
        finish_kernel,
        out_shape=shape(block),
        in_specs=[smem, smem, vmem, vmem, vmem, vmem, vmem],
        out_specs=vmem,
        scratch_shapes=[
            pltpu.VMEM((27, RADIAL, 2, 8, LANES), jnp.float32),
            pltpu.VMEM((9, 2, FRAME, LANES), jnp.float32),
            pltpu.VMEM((27, RADIAL, 2, FRAME, LANES), jnp.float32),
        ],
        compiler_params=params,
        name="finish",
    )(tile_offsets, relax_rates, post, strips, slots, below, above)
    return out[None]


def solution(mesh):
    in_specs = (P("grp", None, None, "az", "ax"), P(), P("ax", None))
    out_specs = P("grp", None, None, "az", "ax")
    return jax.shard_map(local, mesh=mesh, in_specs=in_specs, out_specs=out_specs, check_vma=False)
```

time: 97.8 us -> 47.4 us (0.48); the launches traced: 95.9 us -> 47.2 us
  starting transfers between devices: 41.8 us -> 13.9 us
  blocking collectives: 0 us -> 23.2 us
  matrix products: 15.7 us -> 0 us
  waiting for transfers between devices: 13.1 us -> 0.01 us
  other arithmetic: 10.5 us -> 0 us
  local copies, waits for them, and re-layouts: 11.5 us -> 1.83 us
  Pallas kernels: 0 us -> 8.24 us
  between operations: 3.29 us -> 0.08 us
    all_to_all x0 -> x1, blocking collectives: none -> 23.2 us  [local(): lax.all_to_all(slots, ('grp', 'az'), split_axis=0, concat_axis=0, tiled=T...]
    ppermute x9 -> x2, starting transfers between devices: 33.8 us -> 13.9 us  [the longest x1 9.5 us: local(): above = lax.ppermute(low, 'ax', [(j, i) for i, j in up])]
    dot_general x14 -> x0, matrix products: 15.7 us -> none  [the longest x3 4.36 us: equilibrium(): jnp.einsum('ik,i...->k...', drift_table, state, precision=exact_mode)]
    pallas_call x0 -> x4, Pallas kernels: none -> 8.24 us  [the longest x1 4.07 us: local(): pl.pallas_call(finish_kernel, out_shape=shape(block), in_specs=[smem, sme...]
    ppermute x9 -> x2, waiting for transfers between devices: 8.03 us -> 0.01 us  [the longest x1 0.01 us: local(): below = lax.ppermute(high, 'ax', up)]
    all_to_all x1 -> x0, starting transfers between devices: 7.97 us -> none  [local(): lax.all_to_all(crossed, 'az', split_axis=0, concat_axis=0, tiled=True)]
    all_to_all x1 -> x0, waiting for transfers between devices: 5.03 us -> none  [local(): lax.all_to_all(crossed, 'az', split_axis=0, concat_axis=0, tiled=True)]
    ppermute x5 -> x0, local copies, waits for them, and re-layouts: 3.67 us -> none  [the longest x1 1.65 us: swapped(): lax.ppermute(x, axis, [(i, i ^ 1 << distance) for i in range(lax.axis_siz...]
  transfers between devices with their start and end apart: 10 -> 2, of which waited for: 4 -> 0; matrix products, arithmetic and copies ran while one was open for 11% -> 0% of each run, Pallas kernels for 0% -> 2%
where the time goes in v1:
time: 47.4 us; the launch traced here: 47.2 us
  blocking collectives  23.2 us (49%)
  starting transfers between devices  13.9 us (29%)
  Pallas kernels  8.24 us (17%)
  local copies, waits for them, and re-layouts  1.83 us (4%)
    all_to_all x1, blocking collectives, local(): lax.all_to_all(slots, ('grp', 'az'), split_axis=0, concat_axis=0, tiled=T...  23.2 us
    ppermute x1, starting transfers between devices, local(): above = lax.ppermute(low, 'ax', [(j, i) for i, j in up])  9.5 us
    ppermute x1, starting transfers between devices, local(): below = lax.ppermute(high, 'ax', up)  4.36 us
    pallas_call x1, Pallas kernels, local(): pl.pallas_call(finish_kernel, out_shape=shape(block), in_specs=[smem, sme...  4.07 us
    pallas_call x1, Pallas kernels, local(): pl.pallas_call(fill_kernel, out_shape=(shape(block), shape((2 * COUNT, SL...  2.03 us
    unnamed x8, local copies, waits for them, and re-layouts  1.83 us
    pallas_call x1, Pallas kernels, local(): pl.pallas_call(collide_kernel, out_shape=shape(block), in_specs=[smem, vm...  1.09 us
    pallas_call x1, Pallas kernels, local(): pl.pallas_call(pack_kernel, out_shape=(shape((ROWS, LANES)), shape((ROWS,...  1.05 us
  transfers between devices with their start and end apart: 2, of which 0 were waited for; matrix products, arithmetic and copies ran while one was open for 0% of the time, Pallas kernels for 2%

profile of v1, /device:TPU:1, one launch (start us, length us, event | category | flops | bytes accessed | tf_op | source)
XLA Modules:
  0.0 47.2 jit_solution(8495055916958748281)
XLA Ops:
  0.0 0.0 copy-start.3
  0.0 0.7 %copy-done.3 = s32[1,16]{1,0:T(1,128)S(1)} copy-done((s32[1,16]{1,0:T(1,128)S(1)}, s32[1,16]{1,0:T(1,128)}, u32[]{:S(2)}) %copy-start.3) | copy-done | bytes 88
  0.7 0.0 copy-start
  0.7 1.2 %copy-done = f32[1,27,2,32,128]{4,3,2,1,0:T(8,128)S(1)} copy-done((f32[1,27,2,32,128]{4,3,2,1,0:T(8,128)S(1)}, f32[1,27,2,32,128]{4,3,2,1,0:T(8,128)}, u32[]{:S(2)}) %copy-start) | copy-done | bytes 884760
  1.8 0.0 copy-start.1
  1.8 1.1 %pack.1 = (f32[32,128]{1,0:T(8,128)S(1)}, f32[32,128]{1,0:T(8,128)S(1)}) custom-call(s32[1,16]{1,0:T(1,128)S(1)} %copy-done.3, f32[27,2,32,128]{3,2,1,0:T(8,128)S(1)} %bitcast.2), custom_call_target="tpu_custom_call" | custom-call | tf_op jit(solution)/shard_map/pack/pallas_call | solution.py:364
  2.9 0.0 copy-start.2
  2.9 4.4 %collective-permute-start = (f32[32,128]{1,0:T(8,128)S(1)}, f32[32,128]{1,0:T(8,128)S(1)}, u32[]{:S(2)}, u32[]{:S(2)}) collective-permute-start(f32[32,128]{1,0:T(8,128)S(1)} %get-tuple-element.9), channel_id=1, source_target_pairs={{0,1},{1,2},{2,3},{3,4},{4,5},{5,6},{6,7},{7,8},{8,9},{9,10},{10,1... | collective-permute-start | bytes 49160 | tf_op jit(solution)/shard_map/ppermute | solution.py:374
  7.3 9.5 %collective-permute-start.1 = (f32[32,128]{1,0:T(8,128)S(1)}, f32[32,128]{1,0:T(8,128)S(1)}, u32[]{:S(2)}, u32[]{:S(2)}) collective-permute-start(f32[32,128]{1,0:T(8,128)S(1)} %get-tuple-element.10), channel_id=1, source_target_pairs={{1,0},{2,1},{3,2},{4,3},{5,4},{6,5},{7,6},{8,7},{9,8},{10,9},{11,1... | collective-permute-start | bytes 49160 | tf_op jit(solution)/shard_map/ppermute | solution.py:375
  16.8 0.0 copy-done.1
  16.8 0.0 copy-done.2
  16.8 1.1 %collide.1.post = f32[27,2,32,128]{3,2,1,0:T(8,128)S(1)} custom-call(f32[2,27]{1,0:T(2,128)S(1)} %copy-done.2, f32[27,2,32,128]{3,2,1,0:T(8,128)S(1)} %bitcast.3), custom_call_target="tpu_custom_call" | custom-call | flops 80000000 | bytes 1800000 | tf_op jit(solution)/shard_map/collide/pallas_call | solution.py:376
  17.9 0.0 collective-permute-done.below
  17.9 0.0 collective-permute-done.1.above
  17.9 2.0 %fill.1 = (f32[27,2,32,128]{3,2,1,0:T(8,128)S(1)}, f32[32,48,128]{2,1,0:T(8,128)S(1)}) custom-call(s32[1,16]{1,0:T(1,128)S(1)} %copy-done.3, f32[2,27]{1,0:T(2,128)S(1)} %copy-done.2, f32[27,2,32,128]{3,2,1,0:T(8,128)S(1)} %collide.1.post, f32[32,128]{1,0:T(8,128)S(1)} %collective-permute-done.below, f32[32,128]{1,0:T(8,128)S(1)} %collective-permute-done.1.above), custom_call_target="tpu_custom_call" | custom-call | tf_op jit(solution)/shard_map/fill/pallas_call | solution.py:385
  19.9 23.2 %all_to_all.5.slots = f32[32,48,128]{2,1,0:T(8,128)S(1)} all-to-all(f32[32,48,128]{2,1,0:T(8,128)S(1)} %get-tuple-element.12), channel_id=1, replica_groups=mesh['grp'=2,'az'=16,'ax'=16] {'grp','az'}, dimensions={0} | all-to-all | bytes 1572864 | tf_op jit(solution)/shard_map/all_to_all | solution.py:394
  43.1 4.1 %finish.1 = f32[27,2,32,128]{3,2,1,0:T(8,128)} custom-call(s32[1,16]{1,0:T(1,128)S(1)} %copy-done.3, f32[2,27]{1,0:T(2,128)S(1)} %copy-done.2, f32[27,2,32,128]{3,2,1,0:T(8,128)S(1)} %collide.1.post, f32[27,2,32,128]{3,2,1,0:T(8,128)S(1)} %get-tuple-element.11.strips, f32[32,48,128]{2,1,0:T(8,128)S(1)} %all_to_all.5.slots, ...), custom_call_target="tpu_custom_call" | custom-call | tf_op jit(solution)/shard_map/finish/pallas_call | solution.py:395
Async XLA Ops:
  0.0 0.7 %copy-start.3 = (s32[1,16]{1,0:T(1,128)S(1)}, s32[1,16]{1,0:T(1,128)}, u32[]{:S(2)}) copy-start(s32[1,16]{1,0:T(1,128)} %offsets.5) | copy-start | bytes 196
  0.7 1.2 %copy-start = (f32[1,27,2,32,128]{4,3,2,1,0:T(8,128)S(1)}, f32[1,27,2,32,128]{4,3,2,1,0:T(8,128)}, u32[]{:S(2)}) copy-start(f32[1,27,2,32,128]{4,3,2,1,0:T(8,128)} %param.3) | copy-start | bytes 2654212
  1.8 15.0 %copy-start.1 = (f32[1,27,2,32,128]{4,3,2,1,0:T(8,128)S(1)}, f32[1,27,2,32,128]{4,3,2,1,0:T(8,128)}, u32[]{:S(2)}) copy-start(f32[1,27,2,32,128]{4,3,2,1,0:T(8,128)} %param.3) | copy-start | bytes 2654212
  2.9 13.9 %copy-start.2 = (f32[2,27]{1,0:T(2,128)S(1)}, f32[2,27]{1,0:T(2,128)}, u32[]{:S(2)}) copy-start(f32[2,27]{1,0:T(2,128)} %rates.5) | copy-start | bytes 652
  2.9 15.0 %collective-permute-start = (f32[32,128]{1,0:T(8,128)S(1)}, f32[32,128]{1,0:T(8,128)S(1)}, u32[]{:S(2)}, u32[]{:S(2)}) collective-permute-start(f32[32,128]{1,0:T(8,128)S(1)} %get-tuple-element.9), channel_id=1, source_target_pairs={{0,1},{1,2},{2,3},{3,4},{4,5},{5,6},{6,7},{7,8},{8,9},{9,10},{10,1... | collective-permute-start | bytes 49160 | tf_op jit(solution)/shard_map/ppermute | solution.py:374
  7.3 10.6 %collective-permute-start.1 = (f32[32,128]{1,0:T(8,128)S(1)}, f32[32,128]{1,0:T(8,128)S(1)}, u32[]{:S(2)}, u32[]{:S(2)}) collective-permute-start(f32[32,128]{1,0:T(8,128)S(1)} %get-tuple-element.10), channel_id=1, source_target_pairs={{1,0},{2,1},{3,2},{4,3},{5,4},{6,5},{7,6},{8,7},{9,8},{10,9},{11,1... | collective-permute-start | bytes 49160 | tf_op jit(solution)/shard_map/ppermute | solution.py:375

commit v2 on v1

v2 whole, which is shorter than its diff:
```python
import functools

import jax
import jax.numpy as jnp
from jax import lax
from jax.experimental import pallas as pl
from jax.experimental.pallas import tpu as pltpu
from jax.sharding import PartitionSpec as P


RADIAL, ROWS, FRAME, LANES = 2, 32, 40, 128
COUNT, SLOTS = 16, 2
SLOT_ROWS = 48
CORNERS = 45
EDGE = 36
OFFSET_LANE = 96
TILES = 7
exact_mode = lax.Precision.HIGHEST
speeds = [(cr, ca, cx) for cr in (-1, 0, 1) for ca in (-1, 0, 1) for cx in (-1, 0, 1)]


def at(cr, ca, cx):
    return 9 * (cr + 1) + 3 * (ca + 1) + (cx + 1)


def moments(g):
    for stride in (1, 3, 9):
        out = [None] * 27
        for base in range(27):
            if base // stride % 3 == 0:
                low, mid, high = g[base], g[base + stride], g[base + 2 * stride]
                even = high + low
                out[base] = even + 4.0 * mid
                out[base + stride] = high - low
                out[base + 2 * stride] = even
        g = out
    return g


def balance_moments(m):
    third, ninth = 1.0 / 3.0, 1.0 / 9.0
    rho, jx, ja, jr = m[0], m[1], m[3], m[9]
    inverse = 1.0 / rho
    ur, ua, ux = jr * inverse, ja * inverse, jx * inverse
    rr, aa, xx = jr * ur, ja * ua, jx * ux
    rho3, rho9 = rho * third, rho * ninth
    jr3, ja3, jx3 = jr * third, ja * third, jx * third
    ra, rx, ax = jr * ua, jr * ux, ja * ux
    e = [None] * 27
    e[12], e[10], e[4] = ra, rx, ax
    e[18], e[6], e[2] = rho3 + rr, rho3 + aa, rho3 + xx
    e[21], e[19], e[15], e[11], e[5], e[7] = ja3, jx3, jr3, jr3, ja3, jx3
    e[22], e[16], e[14] = ax * third, rx * third, ra * third
    e[24], e[20], e[8] = rho9 + (rr + aa) * third, rho9 + (rr + xx) * third, rho9 + (aa + xx) * third
    e[25], e[23], e[17] = jx * ninth, ja * ninth, jr * ninth
    e[26] = rho * (1.0 / 27.0) + (rr + aa + xx) * ninth
    return e


def relax(g, rates):
    m = moments(g)
    e = balance_moments(m)
    d = [None] * 27
    for k in range(27):
        if k not in (0, 1, 3, 9):
            d[k] = (m[k] if e[k] is None else m[k] - e[k]) * (rates[k] * 0.125)
    for stride in (1, 3, 9):
        out = [None] * 27
        for base in range(27):
            if base // stride % 3 == 0:
                low, mid, high = d[base], d[base + stride], d[base + 2 * stride]
                out[base] = high if mid is None else high - mid
                out[base + stride] = -0.5 * high if low is None else 0.5 * (low - high)
                out[base + 2 * stride] = high if mid is None else high + mid
        d = out
    return [g[i] - d[i] for i in range(27)]


def face_factor(rates, group):
    fine, coarse = rates[0, 12], rates[1, 12]
    return jnp.where(group == 0, 2.0 * fine / coarse, coarse / (2.0 * fine))


def rescaled(before, after, group, factor):
    m = moments(before)
    rho = m[0] * (1.0 / 216.0)
    inverse = 1.0 / m[0]
    ur, ua, ux = m[9] * inverse, m[3] * inverse, m[1] * inverse
    rest = 1.0 - 1.5 * (ur * ur + ua * ua + ux * ux)
    outward = jnp.where(group == 0, -ur, ur)
    out = []
    for ca in (-1, 0, 1):
        for cx in (-1, 0, 1):
            along = outward
            along = along + ca * ua if ca else along
            along = along + cx * ux if cx else along
            e = rho * (rest + along * (3.0 + 4.5 * along))
            out.append(e + factor * (after[len(out)] - e))
    return out


def halo_entries(annulus, sense):
    out = []
    for depth, ca in ((1, sense), (1, 0), (2, sense)):
        if not annulus and (depth, ca) != (1, sense):
            continue
        for cx in (-1, 0, 1):
            out += [(at(0, ca, cx), 0, depth), (at(0, ca, cx), 1, depth)]
            out += [(at(1, ca, cx), 0, depth), (at(-1, ca, cx), 1, depth)]
    if annulus:
        out += [(at(1, ca, cx), 1, 1) for ca in (-1, 0, 1) for cx in (-1, 0, 1)]
    else:
        out += [(at(-1, sense, cx), 0, 1) for cx in (-1, 0, 1)]
    return out


def lanes_of(rows):
    return lax.broadcasted_iota(jnp.int32, (rows, LANES), 1)


def rows_of(rows, lanes=LANES):
    return lax.broadcasted_iota(jnp.int32, (rows, lanes), 0)


def group_and_place():
    return lax.axis_index("grp"), lax.axis_index("az")


def partner(place, group, offset):
    return (place + (1 - 2 * group) * offset + COUNT) & (COUNT - 1)


def dense_lane(group, r):
    return 4 * (2 * group + r)


def into(acc, tile, lane, first, shift):
    turned = pltpu.roll(tile, shift % LANES, 1) if shift % LANES else tile
    return jnp.where(lane // 4 == first // 4, turned, acc)


def number_kernel(offsets, columns):
    lane = lanes_of(8)
    wide = lax.broadcasted_iota(jnp.int32, (8, COUNT), 1)
    line = jnp.broadcast_to(offsets[...].astype(jnp.float32), (8, COUNT))
    last = jnp.zeros((8, LANES), jnp.float32)
    for g in range(4):
        own = jnp.where(wide == 4 * g + rows_of(8, COUNT) // SLOTS, line, 0.0)
        last = jnp.where(lane == OFFSET_LANE + g, jnp.sum(own, axis=1, keepdims=True), last)
    columns[...] = last


def pack_kernel(columns, pops, message):
    lane = lanes_of(8)
    for i in range(27):
        if i % 4 == 0:
            acc = columns[...] if i == 24 else jnp.zeros((8, LANES), jnp.float32)
        for g in range(4):
            for r in range(RADIAL):
                first = 32 * (i % 4) + dense_lane(g, r)
                acc = into(acc, pops[i, r, 8 * g : 8 * g + 8, :], lane, first, first + 2)
        if i % 4 == 3 or i == 26:
            message[i // 4] = acc


def collide_kernel(offsets, rates, pops, post, slots, face):
    group, place = group_and_place()
    own, other = COUNT * group, COUNT * (1 - group)
    factor = face_factor(rates, group)

    def chunk(step, carry):
        r, rows = step // 4, pl.ds(pl.multiple_of(step % 4 * 8, 8), 8)
        g = [pops[i, r, rows, :] for i in range(27)]
        for i, value in enumerate(relax(g, [rates[group, k] for k in range(27)])):
            post[i, r, rows, :] = value
        return carry

    lax.fori_loop(0, 8, chunk, 0)
    for g in range(4):
        rows = slice(8 * g, 8 * g + 8)
        before = [pops[i, group, rows, :] for i in range(27)]
        after = [post[18 * group + i, group, rows, :] for i in range(9)]
        for i, value in enumerate(rescaled(before, after, group, factor)):
            face[i, rows, :] = value

    def halos(annulus):
        for sense in (1, -1):
            slot = own + ((place + sense + COUNT) & (COUNT - 1))
            for n, (i, r, depth) in enumerate(halo_entries(annulus, sense)):
                row = ROWS - depth if sense == 1 else depth - 1
                slots[slot, n : n + 1, :] = post[i, r, row : row + 1, :]

    @pl.when(group == 0)
    def _():
        halos(True)

    @pl.when(group == 1)
    def _():
        halos(False)

    for q in range(COUNT):
        slot = other + partner(place, group, offsets[0, q])
        for i in range(9):
            slots[slot, 2 * i : 2 * i + 2, :] = face[i, 2 * q : 2 * q + 2, :]
    after = other + ((place - offsets[0, COUNT - 1] + 1 + COUNT) & (COUNT - 1))
    before = other + ((place - offsets[0, 0] - 1 + COUNT) & (COUNT - 1))
    for i in range(9):
        slots[after, 18 + i : 19 + i, :] = face[i, ROWS - 1 : ROWS, :]
        slots[before, 27 + i : 28 + i, :] = face[i, 0:1, :]


def neighbour_offsets(message, width):
    lanes = [message[TILES - 1, :, OFFSET_LANE + g : OFFSET_LANE + g + 1] for g in range(4)]
    return jnp.concatenate([jnp.broadcast_to(x, (8, width)) for x in lanes], 0).astype(jnp.int32)


def edge_kernel(rates, below, above, given, strips, slots, dense, face):
    group, place = group_and_place()
    slots[...] = given[...]
    own, other = COUNT * group, COUNT * (1 - group)
    factor = face_factor(rates, group)
    lane = lanes_of(8)
    merged = [jnp.where(lane % 4 < 2, below[k], above[k]) for k in range(TILES)]
    pops = [pltpu.roll(merged[i // 4], LANES - 32 * (i % 4), 1) if i % 4 else merged[i // 4] for i in range(27)]
    for i, value in enumerate(relax(pops, [rates[group, k] for k in range(27)])):
        dense[i] = value

    def halos(annulus):
        narrow = lax.broadcasted_iota(jnp.int32, (1, LANES), 1)
        for sense in (1, -1):
            slot = own + ((place + sense + COUNT) & (COUNT - 1))
            corners = [jnp.zeros((1, LANES), jnp.float32)] * 2
            for n, (i, r, depth) in enumerate(halo_entries(annulus, sense)):
                g, row = (3, 8 - depth) if sense == 1 else (0, depth - 1)
                shift = 4 * (n % 32) - dense_lane(g, r)
                corners[n // 32] = into(corners[n // 32], dense[i, row : row + 1, :], narrow, 4 * (n % 32), shift)
            for k in range(2):
                slots[slot, CORNERS + k : CORNERS + k + 1, :] = corners[k]

    for i in range(27):
        for r in range(RADIAL):
            for g in range(4):
                shift = LANES - dense_lane(g, r) - 2
                strips[i, r, 8 * g : 8 * g + 8, :] = pltpu.roll(dense[i], shift, 1)

    @pl.when(group == 0)
    def _():
        halos(True)

    @pl.when(group == 1)
    def _():
        halos(False)
        after = [dense[18 + i] for i in range(9)]
        for i, value in enumerate(rescaled(pops, after, group, factor)):
            face[i] = value
        packed = []
        for g in range(4):
            part = jnp.zeros((8, LANES), jnp.float32)
            for i in range(9):
                shift = (2 * i - dense_lane(g, 1) - 1) % LANES
                part = jnp.where(lane // 2 == i, pltpu.roll(face[i], shift, 1) if shift else face[i], part)
            packed.append(part)
        packed = jnp.concatenate(packed, 0)
        wide, row = lanes_of(ROWS), rows_of(ROWS)
        kind, receiver = wide // COUNT, wide % COUNT
        shift = jnp.where(kind == 2, 1, jnp.where(kind == 3, -1, 0))
        fits = ((kind < 2) & (row % 2 == kind)) | ((kind == 2) & (row == ROWS - 1)) | ((kind == 3) & (row == 0))
        picks, values = [], []
        for message, side in ((below, 0), (above, 1)):
            target = (place - neighbour_offsets(message, LANES) + shift + 2 * COUNT) & (COUNT - 1)
            picks.append(jnp.where(fits & (receiver == target), 1.0, 0.0))
            values.append(jnp.where((wide % 2 == side) & (wide < 18), packed, 0.0))
        sent = lax.dot_general(
            jnp.concatenate(picks, 0),
            jnp.concatenate(values, 0),
            (((0,), (0,)), ((), ())),
            precision=exact_mode,
            preferred_element_type=jnp.float32,
        )
        line = sent[0:COUNT]
        for k in range(1, 4):
            line = line + pltpu.roll(sent[COUNT * k : COUNT * (k + 1)], 32 * k, 1)
        for e in range(COUNT):
            slots[other + e, EDGE : EDGE + 1, :] = line[e : e + 1]


def turned_by(tile, shift, axis):
    shift %= tile.shape[axis]
    return pltpu.roll(tile, shift, axis) if shift else tile


def finish_kernel(offsets, rates, post, strips, slots, below, above, out, halo, ghost, mid, side, thin, stage, sems):
    group, place = group_and_place()
    own, other = COUNT * group, COUNT * (1 - group)
    lane = lanes_of(FRAME)

    def halos(annulus):
        for sense in (1, -1):
            slot = own + ((place - sense + COUNT) & (COUNT - 1))
            for n, (i, r, depth) in enumerate(halo_entries(annulus, sense)):
                row = 8 - depth if sense == 1 else depth - 1
                halo[i, r, 0, row : row + 1, :] = slots[slot, n : n + 1, :]
                line = CORNERS + n // 32
                turned = pltpu.roll(slots[slot, line : line + 1, :], (-4 * (n % 32) - 2) % LANES, 1)
                halo[i, r, 1, row : row + 1, :] = turned

    for q in range(COUNT):
        slot = other + partner(place, group, offsets[0, q])
        for i in range(9):
            ghost[i, 0, 2 * q : 2 * q + 2, :] = slots[slot, 2 * i : 2 * i + 2, :]

    def main_of(i, r):
        return jnp.concatenate([post[i, r], halo[i, r, 0]], 0)

    def strip_of(i, r):
        return jnp.concatenate([strips[i, r], halo[i, r, 1]], 0)

    def edged(main, column, cx):
        return jnp.where(lane == (0 if cx == 1 else LANES - 1), column, turned_by(main, cx, 1)) if cx else main

    def send(i):
        if i % 3 == 2:
            pltpu.make_async_copy(stage.at[pl.ds(i - 2, 3)], out.at[pl.ds(i - 2, 3)], sems.at[i // 3]).start()

    @pl.when(group == 1)
    def _():
        halos(False)
        for i, (cr, ca, cx) in enumerate(speeds):
            for r in range(RADIAL):
                if r - cr == RADIAL:
                    stage[i, r] = ghost[i, 0, 0:ROWS]
                else:
                    source = (i - 18, 0) if r - cr == -1 else (i, r - cr)
                    main = edged(main_of(*source), turned_by(strip_of(*source), cx, 1) if cx else None, cx)
                    stage[i, r] = turned_by(main, ca, 0)[0:ROWS]
            send(i)

    @pl.when(group == 0)
    def _():
        halos(True)
        before = other + ((place - 1 + offsets[0, COUNT - 1] + COUNT) & (COUNT - 1))
        after = other + ((place + 1 + offsets[0, 0] + COUNT) & (COUNT - 1))
        for i in range(9):
            ghost[i, 0, FRAME - 1 : FRAME, :] = slots[before, 18 + i : 19 + i, :]
            ghost[i, 0, ROWS : ROWS + 1, :] = slots[after, 27 + i : 28 + i, :]
        received = jnp.concatenate([slots[other + d, EDGE : EDGE + 1, :] for d in range(COUNT)], 0)
        stack = jnp.concatenate([received] + [pltpu.roll(received, LANES - 32 * k, 1) for k in range(1, 4)], 0)
        row, wide = rows_of(FRAME, 64), lax.broadcasted_iota(jnp.int32, (FRAME, 64), 1)
        kind, sender = wide // COUNT, wide % COUNT
        shift = jnp.where(kind == 2, -1, jnp.where(kind == 3, 1, 0))
        fits = ((kind < 2) & (row % 2 == kind) & (row < ROWS)) | ((kind == 2) & (row == FRAME - 1)) | ((kind == 3) & (row == ROWS))
        picked = []
        for message in (below, above):
            offset = neighbour_offsets(message, 64)
            tail = jnp.where(rows_of(8, 64) == 0, offset[0:1], offset[ROWS - 1 : ROWS])
            source = (place + jnp.concatenate([offset, tail], 0) + shift + COUNT) & (COUNT - 1)
            pick = jnp.where(fits & (sender == source), 1.0, 0.0)
            picked.append(
                lax.dot_general(
                    pick, stack, (((1,), (0,)), ((), ())), precision=exact_mode, preferred_element_type=jnp.float32
                )
            )
        columns = jnp.where(lane % 2 == 0, picked[0], picked[1])
        for i in range(9):
            ghost[i, 1] = turned_by(columns, LANES - 1 - 2 * i, 1)

        narrow = lanes_of(8)
        for i, (cr, ca, cx) in enumerate(speeds):
            for r in range(RADIAL):
                if r - cr == -1:
                    main, strip = ghost[i - 18, 0], ghost[i - 18, 1]
                elif r - cr == RADIAL:
                    main, strip = main_of(26 - i, 1), strip_of(26 - i, 1)
                else:
                    main, strip = turned_by(main_of(i, r - cr), ca, 0), turned_by(strip_of(i, r - cr), ca, 0)
                    if cx:
                        near, far = turned_by(main, cx, 1), turned_by(strip, cx, 1)
                        edge = lane == (0 if cx == 1 else LANES - 1)
                        main, strip = jnp.where(edge, far, near), jnp.where(edge, near, far)
                mid[i, r] = main
                side[i, r] = strip

        @pl.when(place >= 0)
        def _():
            for i in range(27):
                dense = jnp.zeros((8, LANES), jnp.float32)
                for r in range(RADIAL):
                    for g in range(5):
                        first = dense_lane(g, r)
                        dense = into(dense, side[i, r, 8 * g : 8 * g + 8, :], narrow, first, first + 2)
                thin[i] = dense

        def chunk(step, carry):
            r, rows = step // 5, pl.ds(pl.multiple_of(step % 5 * 8, 8), 8)
            g = [mid[i, r, rows, :] for i in range(27)]
            for i, value in enumerate(relax(g, [rates[0, k] for k in range(27)])):
                mid[i, r, rows, :] = value
            return carry

        lax.fori_loop(0, 10, chunk, 0)
        for i, value in enumerate(relax([thin[i] for i in range(27)], [rates[0, k] for k in range(27)])):
            thin[i] = value
        for i, (cr, ca, cx) in enumerate(speeds):
            for r in range(RADIAL):
                if r - cr == -1:
                    stage[i, r] = ghost[i - 18, 0, 0:ROWS]
                elif r - cr == RADIAL:
                    stage[i, r] = mid[26 - i, 1, 0:ROWS]
                else:
                    column = None
                    if cx:
                        dense, turn = thin[i], -1 if cx == 1 else LANES - 3
                        column = [turned_by(dense, turn - dense_lane(g, r - cr), 1) for g in range(5)]
                        column = jnp.concatenate(column, 0)
                    stage[i, r] = turned_by(edged(mid[i, r - cr], column, cx), ca, 0)[0:ROWS]
            send(i)

    for k in range(9):
        pltpu.make_async_copy(stage.at[pl.ds(3 * k, 3)], out.at[pl.ds(3 * k, 3)], sems.at[k]).wait()


def local(populations, relax_rates, tile_offsets):
    shape = functools.partial(jax.ShapeDtypeStruct, dtype=jnp.float32)
    block = (27, RADIAL, ROWS, LANES)
    params = pltpu.CompilerParams(vmem_limit_bytes=24 << 20)
    smem, vmem, hbm = [pl.BlockSpec(memory_space=m) for m in (pltpu.SMEM, pltpu.VMEM, pltpu.HBM)]
    columns = pl.pallas_call(
        number_kernel,
        out_shape=shape((8, LANES)),
        in_specs=[vmem],
        out_specs=vmem,
        compiler_params=params,
        cost_estimate=pl.CostEstimate(flops=500_000_000, bytes_accessed=4_000_000, transcendentals=0),
        name="number",
    )(tile_offsets)
    message = pl.pallas_call(
        pack_kernel,
        out_shape=shape((TILES, 8, LANES)),
        in_specs=[vmem, vmem],
        out_specs=vmem,
        compiler_params=params,
        name="pack",
    )(columns, populations[0])
    size = lax.axis_size("ax")
    up = [(i, (i + 1) % size) for i in range(size)]
    below = lax.ppermute(message, "ax", up)
    above = lax.ppermute(message, "ax", [(j, i) for i, j in up])
    post, slots = pl.pallas_call(
        collide_kernel,
        out_shape=(shape(block), shape((2 * COUNT, SLOT_ROWS, LANES))),
        in_specs=[smem, smem, vmem],
        out_specs=(vmem, vmem),
        scratch_shapes=[pltpu.VMEM((9, ROWS, LANES), jnp.float32)],
        compiler_params=params,
        cost_estimate=pl.CostEstimate(flops=80_000_000, bytes_accessed=1_800_000, transcendentals=0),
        name="collide",
    )(tile_offsets, relax_rates, populations[0])
    strips, slots = pl.pallas_call(
        edge_kernel,
        out_shape=(shape(block), shape((2 * COUNT, SLOT_ROWS, LANES))),
        in_specs=[smem, vmem, vmem, vmem],
        out_specs=(vmem, vmem),
        scratch_shapes=[pltpu.VMEM((27, 8, LANES), jnp.float32), pltpu.VMEM((9, 8, LANES), jnp.float32)],
        compiler_params=params,
        name="edge",
    )(relax_rates, below, above, slots)
    slots = lax.all_to_all(slots, ("grp", "az"), split_axis=0, concat_axis=0, tiled=True)
    out = pl.pallas_call(
        finish_kernel,
        out_shape=shape(block),
        in_specs=[smem, smem, vmem, vmem, vmem, vmem, vmem],
        out_specs=hbm,
        scratch_shapes=[
            pltpu.VMEM((27, RADIAL, 2, 8, LANES), jnp.float32),
            pltpu.VMEM((9, 2, FRAME, LANES), jnp.float32),
            pltpu.VMEM((27, RADIAL, FRAME, LANES), jnp.float32),
            pltpu.VMEM((27, RADIAL, FRAME, LANES), jnp.float32),
            pltpu.VMEM((27, 8, LANES), jnp.float32),
            pltpu.VMEM(block, jnp.float32),
            pltpu.SemaphoreType.DMA((9,)),
        ],
        compiler_params=params,
        name="finish",
    )(tile_offsets, relax_rates, post, strips, slots, below, above)
    return out[None]


def solution(mesh):
    in_specs = (P("grp", None, None, "az", "ax"), P(), P("ax", None))
    out_specs = P("grp", None, None, "az", "ax")
    return jax.shard_map(local, mesh=mesh, in_specs=in_specs, out_specs=out_specs, check_vma=False)
```

time: 47.4 us -> 47.7 us (level)
  waiting for transfers between devices: 0.01 us -> 2.54 us
  Pallas kernels: 8.24 us -> 6.18 us
  local copies, waits for them, and re-layouts: 1.83 us -> 1.1 us
  blocking collectives: 23.2 us -> 23.8 us
    ppermute x2, waiting for transfers between devices: 0.01 us -> 2.54 us  [the longest x1 2.53 us: local(): below = lax.ppermute(message, 'ax', up)]
    pallas_call x3 -> x4, Pallas kernels: 4.17 us -> 2.81 us  [the longest x1 1.34 us: local(): pl.pallas_call(collide_kernel, out_shape=(shape(block), shape((2 * COUNT,...]
    unnamed x8 -> x6, local copies, waits for them, and re-layouts: 1.83 us -> 1.1 us
    pallas_call x1, Pallas kernels: 4.07 us -> 3.36 us  [local(): pl.pallas_call(finish_kernel, out_shape=shape(block), in_specs=[smem, sme...]
    all_to_all x1, blocking collectives: 23.2 us -> 23.8 us  [local(): lax.all_to_all(slots, ('grp', 'az'), split_axis=0, concat_axis=0, tiled=T...]
  transfers between devices with their start and end apart: 2 -> 2, of which waited for: 0 -> 1; matrix products, arithmetic and copies ran while one was open for 0% -> 0% of each run, Pallas kernels for 2% -> 3%
where the time goes in v2:
time: 47.7 us; the launch traced here: 47.5 us
  blocking collectives  23.8 us (50%)
  starting transfers between devices  13.9 us (29%)
  Pallas kernels  6.18 us (13%)
  waiting for transfers between devices  2.54 us (5%)
  local copies, waits for them, and re-layouts  1.1 us (2%)
    all_to_all x1, blocking collectives, local(): lax.all_to_all(slots, ('grp', 'az'), split_axis=0, concat_axis=0, tiled=T...  23.8 us
    ppermute x1, starting transfers between devices, local(): above = lax.ppermute(message, 'ax', [(j, i) for i, j in up])  11.9 us
    pallas_call x1, Pallas kernels, local(): pl.pallas_call(finish_kernel, out_shape=shape(block), in_specs=[smem, sme...  3.36 us
    ppermute x1, waiting for transfers between devices, local(): below = lax.ppermute(message, 'ax', up)  2.53 us
    ppermute x1, starting transfers between devices, local(): below = lax.ppermute(message, 'ax', up)  1.92 us
    pallas_call x1, Pallas kernels, local(): pl.pallas_call(collide_kernel, out_shape=(shape(block), shape((2 * COUNT,...  1.34 us
    pallas_call x1, Pallas kernels, local(): pl.pallas_call(edge_kernel, out_shape=(shape(block), shape((2 * COUNT, SL...  1.11 us
    unnamed x6, local copies, waits for them, and re-layouts  1.1 us
  transfers between devices with their start and end apart: 2, of which 1 were waited for; matrix products, arithmetic and copies ran while one was open for 0% of the time, Pallas kernels for 3%

profile of v2, /device:TPU:1, one launch (start us, length us, event | category | flops | bytes accessed | tf_op | source)
XLA Modules:
  0.0 47.5 jit_solution(3892289631173663731)
XLA Ops:
  0.0 0.0 copy-start
  0.0 0.0 copy-start.2
  0.0 0.7 %copy-done.2 = s32[1,16]{1,0:T(1,128)S(1)} copy-done((s32[1,16]{1,0:T(1,128)S(1)}, s32[1,16]{1,0:T(1,128)}, u32[]{:S(2)}) %copy-start.2) | copy-done | bytes 88
  0.7 0.1 number.1.columns
  0.8 0.4 copy-done
  1.2 0.0 copy-start.1
  1.2 0.3 pack.1
  1.5 11.9 %collective-permute-start.1 = (f32[7,8,128]{2,1,0:T(8,128)S(1)}, f32[7,8,128]{2,1,0:T(8,128)S(1)}, u32[]{:S(2)}, u32[]{:S(2)}) collective-permute-start(f32[7,8,128]{2,1,0:T(8,128)S(1)} %pack.1), channel_id=1, source_target_pairs={{1,0},{2,1},{3,2},{4,3},{5,4},{6,5},{7,6},{8,7},{9,8},{10,9},{11,1... | collective-permute-start | bytes 86024 | tf_op jit(solution)/shard_map/ppermute | solution.py:447
  13.4 1.9 %collective-permute-start = (f32[7,8,128]{2,1,0:T(8,128)S(1)}, f32[7,8,128]{2,1,0:T(8,128)S(1)}, u32[]{:S(2)}, u32[]{:S(2)}) collective-permute-start(f32[7,8,128]{2,1,0:T(8,128)S(1)} %pack.1), channel_id=1, source_target_pairs={{0,1},{1,2},{2,3},{3,4},{4,5},{5,6},{6,7},{7,8},{8,9},{9,10},{10,1... | collective-permute-start | bytes 86024 | tf_op jit(solution)/shard_map/ppermute | solution.py:446
  15.4 0.0 copy-done.1
  15.4 1.3 %collide.1 = (f32[27,2,32,128]{3,2,1,0:T(8,128)S(1)}, f32[32,48,128]{2,1,0:T(8,128)S(1)}) custom-call(s32[1,16]{1,0:T(1,128)S(1)} %copy-done.2, f32[2,27]{1,0:T(2,128)S(1)} %copy-done.1, f32[27,2,32,128]{3,2,1,0:T(8,128)S(1)} %bitcast.3), custom_call_target="tpu_custom_call" | custom-call | flops 80000000 | bytes 1800000 | tf_op jit(solution)/shard_map/collide/pallas_call | solution.py:448
  16.7 0.0 collective-permute-done.1.above
  16.7 2.5 %collective-permute-done.below = f32[7,8,128]{2,1,0:T(8,128)S(1)} collective-permute-done((f32[7,8,128]{2,1,0:T(8,128)S(1)}, f32[7,8,128]{2,1,0:T(8,128)S(1)}, u32[]{:S(2)}, u32[]{:S(2)}) %collective-permute-start) | collective-permute-done | bytes 28704 | tf_op jit(solution)/shard_map/ppermute | solution.py:446
  19.3 1.1 %edge.1 = (f32[27,2,32,128]{3,2,1,0:T(8,128)S(1)}, f32[32,48,128]{2,1,0:T(8,128)S(1)}) custom-call(f32[2,27]{1,0:T(2,128)S(1)} %copy-done.1, f32[7,8,128]{2,1,0:T(8,128)S(1)} %collective-permute-done.below, f32[7,8,128]{2,1,0:T(8,128)S(1)} %collective-permute-done.1.above, f32[32,48,128]{2,1,0:T(8,128)S(1)} %get-tuple-element.10.given), custom_call_target="tpu_custom_call" | custom-call | tf_op jit(solution)/shard_map/edge/pallas_call | solution.py:458
  20.4 23.8 %all_to_all.5.slots = f32[32,48,128]{2,1,0:T(8,128)S(1)} all-to-all(f32[32,48,128]{2,1,0:T(8,128)S(1)} %get-tuple-element.12), channel_id=1, replica_groups=mesh['grp'=2,'az'=16,'ax'=16] {'grp','az'}, dimensions={0} | all-to-all | bytes 1572864 | tf_op jit(solution)/shard_map/all_to_all | solution.py:467
  44.1 3.4 %finish.1 = f32[27,2,32,128]{3,2,1,0:T(8,128)} custom-call(s32[1,16]{1,0:T(1,128)S(1)} %copy-done.2, f32[2,27]{1,0:T(2,128)S(1)} %copy-done.1, f32[27,2,32,128]{3,2,1,0:T(8,128)S(1)} %get-tuple-element.9.post, f32[27,2,32,128]{3,2,1,0:T(8,128)S(1)} %get-tuple-element.11.strips, f32[32,48,128]{2,1,0:T(8,128)S(1)} %all_to_all.5.slots, ...), custom_call_target="tpu_custom_call" | custom-call | tf_op jit(solution)/shard_map/finish/pallas_call | solution.py:468
Async XLA Ops:
  0.0 1.2 %copy-start = (f32[1,27,2,32,128]{4,3,2,1,0:T(8,128)S(1)}, f32[1,27,2,32,128]{4,3,2,1,0:T(8,128)}, u32[]{:S(2)}) copy-start(f32[1,27,2,32,128]{4,3,2,1,0:T(8,128)} %param.3) | copy-start | bytes 2654212
  0.0 0.7 %copy-start.2 = (s32[1,16]{1,0:T(1,128)S(1)}, s32[1,16]{1,0:T(1,128)}, u32[]{:S(2)}) copy-start(s32[1,16]{1,0:T(1,128)} %offsets.5) | copy-start | bytes 196
  1.2 14.2 %copy-start.1 = (f32[2,27]{1,0:T(2,128)S(1)}, f32[2,27]{1,0:T(2,128)}, u32[]{:S(2)}) copy-start(f32[2,27]{1,0:T(2,128)} %rates.5) | copy-start | bytes 652
  1.5 15.2 %collective-permute-start.1 = (f32[7,8,128]{2,1,0:T(8,128)S(1)}, f32[7,8,128]{2,1,0:T(8,128)S(1)}, u32[]{:S(2)}, u32[]{:S(2)}) collective-permute-start(f32[7,8,128]{2,1,0:T(8,128)S(1)} %pack.1), channel_id=1, source_target_pairs={{1,0},{2,1},{3,2},{4,3},{5,4},{6,5},{7,6},{8,7},{9,8},{10,9},{11,1... | collective-permute-start | bytes 86024 | tf_op jit(solution)/shard_map/ppermute | solution.py:447
  13.4 5.8 %collective-permute-start = (f32[7,8,128]{2,1,0:T(8,128)S(1)}, f32[7,8,128]{2,1,0:T(8,128)S(1)}, u32[]{:S(2)}, u32[]{:S(2)}) collective-permute-start(f32[7,8,128]{2,1,0:T(8,128)S(1)} %pack.1), channel_id=1, source_target_pairs={{0,1},{1,2},{2,3},{3,4},{4,5},{5,6},{6,7},{7,8},{8,9},{9,10},{10,1... | collective-permute-start | bytes 86024 | tf_op jit(solution)/shard_map/ppermute | solution.py:446

commit v3 on v2

--- a/solution.py
+++ b/solution.py
@@ -10,8 +10,9 @@
 
 RADIAL, ROWS, FRAME, LANES = 2, 32, 40, 128
 COUNT, SLOTS = 16, 2
-SLOT_ROWS = 48
-CORNERS = 45
+SLOT_ROWS = 40
+SUMS = 30
+CORNERS = 36
 EDGE = 36
 OFFSET_LANE = 96
 TILES = 7
@@ -101,19 +102,31 @@
 
 def halo_entries(annulus, sense):
     out = []
-    for depth, ca in ((1, sense), (1, 0), (2, sense)):
-        if not annulus and (depth, ca) != (1, sense):
-            continue
+    for depth in (1, 2) if annulus else (1,):
         for cx in (-1, 0, 1):
-            out += [(at(0, ca, cx), 0, depth), (at(0, ca, cx), 1, depth)]
-            out += [(at(1, ca, cx), 0, depth), (at(-1, ca, cx), 1, depth)]
+            out += [(at(0, sense, cx), 0, depth), (at(0, sense, cx), 1, depth)]
+            out += [(at(1, sense, cx), 0, depth), (at(-1, sense, cx), 1, depth)]
     if annulus:
-        out += [(at(1, ca, cx), 1, 1) for ca in (-1, 0, 1) for cx in (-1, 0, 1)]
+        out += [(at(1, ca, cx), 1, 1) for ca in (-1, 1) for cx in (-1, 0, 1)]
     else:
         out += [(at(-1, sense, cx), 0, 1) for cx in (-1, 0, 1)]
     return out
 
 
+stand_ins = [(at(0, 0, 0), 0), (at(0, 0, 1), 0), (at(-1, 0, 0), 0), (at(0, 0, 0), 1), (at(0, 0, 1), 1), (at(1, 0, 0), 1)]
+
+
+def stand_in_values(p0, q0, p1, r1, q1):
+    quarter = 0.25
+    along0 = (p0[2] - p0[0]) + quarter * (q0[2] - q0[0])
+    still0 = p0[1] + quarter * (p0[2] + p0[0] - along0)
+    inward0 = q0[1] + quarter * (q0[2] + q0[0])
+    plus, minus = r1[1] + quarter * (r1[2] + r1[0]), q1[1] + quarter * (q1[2] + q1[0])
+    along1 = (p1[2] - p1[0]) + quarter * ((r1[2] - r1[0]) + (q1[2] - q1[0]))
+    still1 = p1[1] + quarter * (p1[2] + p1[0] - along1) + 0.5 * minus
+    return [still0, along0, inward0, still1, along1, plus - minus]
+
+
 def lanes_of(rows):
     return lax.broadcasted_iota(jnp.int32, (rows, LANES), 1)
 
@@ -132,6 +145,11 @@
 
 def dense_lane(group, r):
     return 4 * (2 * group + r)
+
+
+def turned_by(tile, shift, axis):
+    shift %= tile.shape[axis]
+    return pltpu.roll(tile, shift, axis) if shift else tile
 
 
 def into(acc, tile, lane, first, shift):
@@ -214,7 +232,27 @@
     return jnp.concatenate([jnp.broadcast_to(x, (8, width)) for x in lanes], 0).astype(jnp.int32)
 
 
-def edge_kernel(rates, below, above, given, strips, slots, dense, face):
+def halo_sums(post, strips, group):
+    rows, lane = slice(8 * group, 8 * group + 8), lanes_of(8)
+
+    def moved(cr, r):
+        out = []
+        for cx in (-1, 0, 1):
+            main, strip = post[at(cr, 0, cx), r, rows, :], strips[at(cr, 0, cx), r, rows, :]
+            if cx:
+                near, far = turned_by(main, cx, 1), turned_by(strip, cx, 1)
+                edge = lane == (0 if cx == 1 else LANES - 1)
+                main, strip = jnp.where(edge, far, near), jnp.where(edge, near, far)
+            out.append((main, strip))
+        return out
+
+    back = [(post[at(1, 0, -cx), 1, rows, :], strips[at(1, 0, -cx), 1, rows, :]) for cx in (-1, 0, 1)]
+    parts = [moved(0, 0), moved(-1, 1), moved(0, 1), moved(1, 0), back]
+    main, strip = [stand_in_values(*[[value[k] for value in part] for part in parts]) for k in (0, 1)]
+    return list(zip(main, strip))
+
+
+def edge_kernel(rates, post, below, above, given, strips, slots, dense, face):
     group, place = group_and_place()
     slots[...] = given[...]
     own, other = COUNT * group, COUNT * (1 - group)
@@ -234,6 +272,12 @@
                 g, row = (3, 8 - depth) if sense == 1 else (0, depth - 1)
                 shift = 4 * (n % 32) - dense_lane(g, r)
                 corners[n // 32] = into(corners[n // 32], dense[i, row : row + 1, :], narrow, 4 * (n % 32), shift)
+            if annulus:
+                row = 7 if sense == 1 else 0
+                for n, (main, strip) in enumerate(halo_sums(post, strips, 3 if sense == 1 else 0), SUMS):
+                    slots[slot, n : n + 1, :] = main[row : row + 1]
+                    shift = (4 * (n % 32) + 2) % LANES
+                    corners[n // 32] = into(corners[n // 32], strip[row : row + 1], narrow, 4 * (n % 32), shift)
             for k in range(2):
                 slots[slot, CORNERS + k : CORNERS + k + 1, :] = corners[k]
 
@@ -284,12 +328,7 @@
             slots[other + e, EDGE : EDGE + 1, :] = line[e : e + 1]
 
 
-def turned_by(tile, shift, axis):
-    shift %= tile.shape[axis]
-    return pltpu.roll(tile, shift, axis) if shift else tile
-
-
-def finish_kernel(offsets, rates, post, strips, slots, below, above, out, halo, ghost, mid, side, thin, stage, sems):
+def finish_kernel(offsets, rates, post, strips, slots, below, above, out, halo, stand, ghost, mid, side, thin, stage, sems):
     group, place = group_and_place()
     own, other = COUNT * group, COUNT * (1 - group)
     lane = lanes_of(FRAME)
@@ -303,6 +342,13 @@
                 line = CORNERS + n // 32
                 turned = pltpu.roll(slots[slot, line : line + 1, :], (-4 * (n % 32) - 2) % LANES, 1)
                 halo[i, r, 1, row : row + 1, :] = turned
+            if annulus:
+                for n in range(SUMS, SUMS + 6):
+                    row = 7 if sense == 1 else 0
+                    stand[n - SUMS, 0, row : row + 1, :] = slots[slot, n : n + 1, :]
+                    line = CORNERS + n // 32
+                    turned = pltpu.roll(slots[slot, line : line + 1, :], (-4 * (n % 32) - 2) % LANES, 1)
+                    stand[n - SUMS, 1, row : row + 1, :] = turned
 
     for q in range(COUNT):
         slot = other + partner(place, group, offsets[0, q])
@@ -364,7 +410,7 @@
         for i in range(9):
             ghost[i, 1] = turned_by(columns, LANES - 1 - 2 * i, 1)
 
-        narrow = lanes_of(8)
+        narrow, none = lanes_of(8), jnp.zeros((8, LANES), jnp.float32)
         for i, (cr, ca, cx) in enumerate(speeds):
             for r in range(RADIAL):
                 if r - cr == -1:
@@ -377,8 +423,15 @@
                         near, far = turned_by(main, cx, 1), turned_by(strip, cx, 1)
                         edge = lane == (0 if cx == 1 else LANES - 1)
                         main, strip = jnp.where(edge, far, near), jnp.where(edge, near, far)
-                mid[i, r] = main
-                side[i, r] = strip
+                if ca or r - cr == -1:
+                    mid[i, r] = main
+                    side[i, r] = strip
+                else:
+                    mid[i, r, 0:ROWS] = main[0:ROWS]
+                    side[i, r, 0:ROWS] = strip[0:ROWS]
+                    given = (i, r) in stand_ins
+                    mid[i, r, ROWS:FRAME] = stand[stand_ins.index((i, r)), 0] if given else none
+                    side[i, r, ROWS:FRAME] = stand[stand_ins.index((i, r)), 1] if given else none
 
         @pl.when(place >= 0)
         def _():
@@ -458,12 +511,12 @@
     strips, slots = pl.pallas_call(
         edge_kernel,
         out_shape=(shape(block), shape((2 * COUNT, SLOT_ROWS, LANES))),
-        in_specs=[smem, vmem, vmem, vmem],
+        in_specs=[smem, vmem, vmem, vmem, vmem],
         out_specs=(vmem, vmem),
         scratch_shapes=[pltpu.VMEM((27, 8, LANES), jnp.float32), pltpu.VMEM((9, 8, LANES), jnp.float32)],
         compiler_params=params,
         name="edge",
-    )(relax_rates, below, above, slots)
+    )(relax_rates, post, below, above, slots)
     slots = lax.all_to_all(slots, ("grp", "az"), split_axis=0, concat_axis=0, tiled=True)
     out = pl.pallas_call(
         finish_kernel,
@@ -472,6 +525,7 @@
         out_specs=hbm,
         scratch_shapes=[
             pltpu.VMEM((27, RADIAL, 2, 8, LANES), jnp.float32),
+            pltpu.VMEM((6, 2, 8, LANES), jnp.float32),
             pltpu.VMEM((9, 2, FRAME, LANES), jnp.float32),
             pltpu.VMEM((27, RADIAL, FRAME, LANES), jnp.float32),
             pltpu.VMEM((27, RADIAL, FRAME, LANES), jnp.float32),

time: 47.7 us -> 46.2 us (0.969)
  blocking collectives: 23.8 us -> 22.4 us
    all_to_all x1, blocking collectives: 23.8 us -> 22.4 us  [local(): lax.all_to_all(slots, ('grp', 'az'), split_axis=0, concat_axis=0, tiled=T...]
where the time goes in v3:
time: 46.2 us; the launch traced here: 46 us
  blocking collectives  22.4 us (48%)
  starting transfers between devices  13.9 us (30%)
  Pallas kernels  6.13 us (13%)
  waiting for transfers between devices  2.55 us (6%)
  local copies, waits for them, and re-layouts  1.1 us (2%)
    all_to_all x1, blocking collectives, local(): lax.all_to_all(slots, ('grp', 'az'), split_axis=0, concat_axis=0, tiled=T...  22.4 us
    ppermute x1, starting transfers between devices, local(): above = lax.ppermute(message, 'ax', [(j, i) for i, j in up])  11.9 us
    pallas_call x1, Pallas kernels, local(): pl.pallas_call(finish_kernel, out_shape=shape(block), in_specs=[smem, sme...  3.31 us
    ppermute x1, waiting for transfers between devices, local(): below = lax.ppermute(message, 'ax', up)  2.54 us
    ppermute x1, starting transfers between devices, local(): below = lax.ppermute(message, 'ax', up)  1.92 us
    pallas_call x1, Pallas kernels, local(): pl.pallas_call(collide_kernel, out_shape=(shape(block), shape((2 * COUNT,...  1.32 us
    pallas_call x1, Pallas kernels, local(): pl.pallas_call(edge_kernel, out_shape=(shape(block), shape((2 * COUNT, SL...  1.13 us
    unnamed x6, local copies, waits for them, and re-layouts  1.1 us
  transfers between devices with their start and end apart: 2, of which 1 were waited for; matrix products, arithmetic and copies ran while one was open for 0% of the time, Pallas kernels for 3%

profile of v3, /device:TPU:1, one launch (start us, length us, event | category | flops | bytes accessed | tf_op | source)
XLA Modules:
  0.0 46.0 jit_solution(13157112986412704837)
XLA Ops:
  0.0 0.0 copy-start
  0.0 0.0 copy-start.2
  0.0 0.7 %copy-done.2 = s32[1,16]{1,0:T(1,128)S(1)} copy-done((s32[1,16]{1,0:T(1,128)S(1)}, s32[1,16]{1,0:T(1,128)}, u32[]{:S(2)}) %copy-start.2) | copy-done | bytes 88
  0.7 0.1 number.1.columns
  0.8 0.4 copy-done
  1.2 0.0 copy-start.1
  1.2 0.3 pack.1
  1.5 11.9 %collective-permute-start.1 = (f32[7,8,128]{2,1,0:T(8,128)S(1)}, f32[7,8,128]{2,1,0:T(8,128)S(1)}, u32[]{:S(2)}, u32[]{:S(2)}) collective-permute-start(f32[7,8,128]{2,1,0:T(8,128)S(1)} %pack.1), channel_id=1, source_target_pairs={{1,0},{2,1},{3,2},{4,3},{5,4},{6,5},{7,6},{8,7},{9,8},{10,9},{11,1... | collective-permute-start | bytes 86024 | tf_op jit(solution)/shard_map/ppermute | solution.py:500
  13.4 1.9 %collective-permute-start = (f32[7,8,128]{2,1,0:T(8,128)S(1)}, f32[7,8,128]{2,1,0:T(8,128)S(1)}, u32[]{:S(2)}, u32[]{:S(2)}) collective-permute-start(f32[7,8,128]{2,1,0:T(8,128)S(1)} %pack.1), channel_id=1, source_target_pairs={{0,1},{1,2},{2,3},{3,4},{4,5},{5,6},{6,7},{7,8},{8,9},{9,10},{10,1... | collective-permute-start | bytes 86024 | tf_op jit(solution)/shard_map/ppermute | solution.py:499
  15.4 0.0 copy-done.1
  15.4 1.3 %collide.1 = (f32[27,2,32,128]{3,2,1,0:T(8,128)S(1)}, f32[32,40,128]{2,1,0:T(8,128)S(1)}) custom-call(s32[1,16]{1,0:T(1,128)S(1)} %copy-done.2, f32[2,27]{1,0:T(2,128)S(1)} %copy-done.1, f32[27,2,32,128]{3,2,1,0:T(8,128)S(1)} %bitcast.3), custom_call_target="tpu_custom_call" | custom-call | flops 80000000 | bytes 1800000 | tf_op jit(solution)/shard_map/collide/pallas_call | solution.py:501
  16.7 0.0 collective-permute-done.1.above
  16.7 2.5 %collective-permute-done.below = f32[7,8,128]{2,1,0:T(8,128)S(1)} collective-permute-done((f32[7,8,128]{2,1,0:T(8,128)S(1)}, f32[7,8,128]{2,1,0:T(8,128)S(1)}, u32[]{:S(2)}, u32[]{:S(2)}) %collective-permute-start) | collective-permute-done | bytes 28704 | tf_op jit(solution)/shard_map/ppermute | solution.py:499
  19.3 1.1 %edge.1 = (f32[27,2,32,128]{3,2,1,0:T(8,128)S(1)}, f32[32,40,128]{2,1,0:T(8,128)S(1)}) custom-call(f32[2,27]{1,0:T(2,128)S(1)} %copy-done.1, f32[27,2,32,128]{3,2,1,0:T(8,128)S(1)} %get-tuple-element.9.post, f32[7,8,128]{2,1,0:T(8,128)S(1)} %collective-permute-done.below, f32[7,8,128]{2,1,0:T(8,128)S(1)} %collective-permute-done.1.above, ...), custom_call_target="tpu_custom_call" | custom-call | tf_op jit(solution)/shard_map/edge/pallas_call | solution.py:511
  20.4 22.4 %all_to_all.5.slots = f32[32,40,128]{2,1,0:T(8,128)S(1)} all-to-all(f32[32,40,128]{2,1,0:T(8,128)S(1)} %get-tuple-element.12), channel_id=1, replica_groups=mesh['grp'=2,'az'=16,'ax'=16] {'grp','az'}, dimensions={0} | all-to-all | bytes 1310720 | tf_op jit(solution)/shard_map/all_to_all | solution.py:520
  42.7 3.3 %finish.1 = f32[27,2,32,128]{3,2,1,0:T(8,128)} custom-call(s32[1,16]{1,0:T(1,128)S(1)} %copy-done.2, f32[2,27]{1,0:T(2,128)S(1)} %copy-done.1, f32[27,2,32,128]{3,2,1,0:T(8,128)S(1)} %get-tuple-element.9.post, f32[27,2,32,128]{3,2,1,0:T(8,128)S(1)} %get-tuple-element.11.strips, f32[32,40,128]{2,1,0:T(8,128)S(1)} %all_to_all.5.slots, ...), custom_call_target="tpu_custom_call" | custom-call | tf_op jit(solution)/shard_map/finish/pallas_call | solution.py:521
Async XLA Ops:
  0.0 1.2 %copy-start = (f32[1,27,2,32,128]{4,3,2,1,0:T(8,128)S(1)}, f32[1,27,2,32,128]{4,3,2,1,0:T(8,128)}, u32[]{:S(2)}) copy-start(f32[1,27,2,32,128]{4,3,2,1,0:T(8,128)} %param.3) | copy-start | bytes 2654212
  0.0 0.7 %copy-start.2 = (s32[1,16]{1,0:T(1,128)S(1)}, s32[1,16]{1,0:T(1,128)}, u32[]{:S(2)}) copy-start(s32[1,16]{1,0:T(1,128)} %offsets.5) | copy-start | bytes 196
  1.2 14.2 %copy-start.1 = (f32[2,27]{1,0:T(2,128)S(1)}, f32[2,27]{1,0:T(2,128)}, u32[]{:S(2)}) copy-start(f32[2,27]{1,0:T(2,128)} %rates.5) | copy-start | bytes 652
  1.5 15.2 %collective-permute-start.1 = (f32[7,8,128]{2,1,0:T(8,128)S(1)}, f32[7,8,128]{2,1,0:T(8,128)S(1)}, u32[]{:S(2)}, u32[]{:S(2)}) collective-permute-start(f32[7,8,128]{2,1,0:T(8,128)S(1)} %pack.1), channel_id=1, source_target_pairs={{1,0},{2,1},{3,2},{4,3},{5,4},{6,5},{7,6},{8,7},{9,8},{10,9},{11,1... | collective-permute-start | bytes 86024 | tf_op jit(solution)/shard_map/ppermute | solution.py:500
  13.4 5.8 %collective-permute-start = (f32[7,8,128]{2,1,0:T(8,128)S(1)}, f32[7,8,128]{2,1,0:T(8,128)S(1)}, u32[]{:S(2)}, u32[]{:S(2)}) collective-permute-start(f32[7,8,128]{2,1,0:T(8,128)S(1)} %pack.1), channel_id=1, source_target_pairs={{0,1},{1,2},{2,3},{3,4},{4,5},{5,6},{6,7},{7,8},{8,9},{9,10},{10,1... | collective-permute-start | bytes 86024 | tf_op jit(solution)/shard_map/ppermute | solution.py:499

commit v4 on v3

--- a/solution.py
+++ b/solution.py
@@ -64,7 +64,7 @@
     d = [None] * 27
     for k in range(27):
         if k not in (0, 1, 3, 9):
-            d[k] = (m[k] if e[k] is None else m[k] - e[k]) * (rates[k] * 0.125)
+            d[k] = (m[k] if e[k] is None else m[k] - e[k]) * rates[k]
     for stride in (1, 3, 9):
         out = [None] * 27
         for base in range(27):
@@ -181,15 +181,18 @@
             message[i // 4] = acc
 
 
-def collide_kernel(offsets, rates, pops, post, slots, face):
+def collide_kernel(offsets, rates, pops, post, slots, scales, face):
     group, place = group_and_place()
     own, other = COUNT * group, COUNT * (1 - group)
     factor = face_factor(rates, group)
+    scaled = [rates[group, k] * 0.125 for k in range(27)]
+    for k, value in enumerate(scaled + [factor]):
+        scales[k] = jnp.full((8, LANES), value, jnp.float32)
 
     def chunk(step, carry):
         r, rows = step // 4, pl.ds(pl.multiple_of(step % 4 * 8, 8), 8)
         g = [pops[i, r, rows, :] for i in range(27)]
-        for i, value in enumerate(relax(g, [rates[group, k] for k in range(27)])):
+        for i, value in enumerate(relax(g, scaled)):
             post[i, r, rows, :] = value
         return carry
 
@@ -252,15 +255,15 @@
     return list(zip(main, strip))
 
 
-def edge_kernel(rates, post, below, above, given, strips, slots, dense, face):
+def edge_kernel(scales, post, below, above, given, strips, slots, dense, face):
     group, place = group_and_place()
     slots[...] = given[...]
     own, other = COUNT * group, COUNT * (1 - group)
-    factor = face_factor(rates, group)
+    factor = scales[27]
     lane = lanes_of(8)
     merged = [jnp.where(lane % 4 < 2, below[k], above[k]) for k in range(TILES)]
     pops = [pltpu.roll(merged[i // 4], LANES - 32 * (i % 4), 1) if i % 4 else merged[i // 4] for i in range(27)]
-    for i, value in enumerate(relax(pops, [rates[group, k] for k in range(27)])):
+    for i, value in enumerate(relax(pops, [scales[k] for k in range(27)])):
         dense[i] = value
 
     def halos(annulus):
@@ -328,7 +331,9 @@
             slots[other + e, EDGE : EDGE + 1, :] = line[e : e + 1]
 
 
-def finish_kernel(offsets, rates, post, strips, slots, below, above, out, halo, stand, ghost, mid, side, thin, stage, sems):
+def finish_kernel(numbers, scales, post, strips, slots, below, above, out, halo, stand, ghost, mid, side, thin, stage, offsets, sems, small):
+    fetch = pltpu.make_async_copy(numbers, offsets, small)
+    fetch.start()
     group, place = group_and_place()
     own, other = COUNT * group, COUNT * (1 - group)
     lane = lanes_of(FRAME)
@@ -350,6 +355,15 @@
                     turned = pltpu.roll(slots[slot, line : line + 1, :], (-4 * (n % 32) - 2) % LANES, 1)
                     stand[n - SUMS, 1, row : row + 1, :] = turned
 
+    @pl.when(group == 1)
+    def _():
+        halos(False)
+
+    @pl.when(group == 0)
+    def _():
+        halos(True)
+
+    fetch.wait()
     for q in range(COUNT):
         slot = other + partner(place, group, offsets[0, q])
         for i in range(9):
@@ -370,7 +384,6 @@
 
     @pl.when(group == 1)
     def _():
-        halos(False)
         for i, (cr, ca, cx) in enumerate(speeds):
             for r in range(RADIAL):
                 if r - cr == RADIAL:
@@ -383,7 +396,6 @@
 
     @pl.when(group == 0)
     def _():
-        halos(True)
         before = other + ((place - 1 + offsets[0, COUNT - 1] + COUNT) & (COUNT - 1))
         after = other + ((place + 1 + offsets[0, 0] + COUNT) & (COUNT - 1))
         for i in range(9):
@@ -446,12 +458,12 @@
         def chunk(step, carry):
             r, rows = step // 5, pl.ds(pl.multiple_of(step % 5 * 8, 8), 8)
             g = [mid[i, r, rows, :] for i in range(27)]
-            for i, value in enumerate(relax(g, [rates[0, k] for k in range(27)])):
+            for i, value in enumerate(relax(g, [scales[k] for k in range(27)])):
                 mid[i, r, rows, :] = value
             return carry
 
         lax.fori_loop(0, 10, chunk, 0)
-        for i, value in enumerate(relax([thin[i] for i in range(27)], [rates[0, k] for k in range(27)])):
+        for i, value in enumerate(relax([thin[i] for i in range(27)], [scales[k] for k in range(27)])):
             thin[i] = value
         for i, (cr, ca, cx) in enumerate(speeds):
             for r in range(RADIAL):
@@ -498,11 +510,11 @@
     up = [(i, (i + 1) % size) for i in range(size)]
     below = lax.ppermute(message, "ax", up)
     above = lax.ppermute(message, "ax", [(j, i) for i, j in up])
-    post, slots = pl.pallas_call(
+    post, slots, scales = pl.pallas_call(
         collide_kernel,
-        out_shape=(shape(block), shape((2 * COUNT, SLOT_ROWS, LANES))),
+        out_shape=(shape(block), shape((2 * COUNT, SLOT_ROWS, LANES)), shape((28, 8, LANES))),
         in_specs=[smem, smem, vmem],
-        out_specs=(vmem, vmem),
+        out_specs=(vmem, vmem, vmem),
         scratch_shapes=[pltpu.VMEM((9, ROWS, LANES), jnp.float32)],
         compiler_params=params,
         cost_estimate=pl.CostEstimate(flops=80_000_000, bytes_accessed=1_800_000, transcendentals=0),
@@ -511,17 +523,17 @@
     strips, slots = pl.pallas_call(
         edge_kernel,
         out_shape=(shape(block), shape((2 * COUNT, SLOT_ROWS, LANES))),
-        in_specs=[smem, vmem, vmem, vmem, vmem],
+        in_specs=[vmem] * 5,
         out_specs=(vmem, vmem),
         scratch_shapes=[pltpu.VMEM((27, 8, LANES), jnp.float32), pltpu.VMEM((9, 8, LANES), jnp.float32)],
         compiler_params=params,
         name="edge",
-    )(relax_rates, post, below, above, slots)
+    )(scales, post, below, above, slots)
     slots = lax.all_to_all(slots, ("grp", "az"), split_axis=0, concat_axis=0, tiled=True)
     out = pl.pallas_call(
         finish_kernel,
         out_shape=shape(block),
-        in_specs=[smem, smem, vmem, vmem, vmem, vmem, vmem],
+        in_specs=[hbm] + [vmem] * 6,
         out_specs=hbm,
         scratch_shapes=[
             pltpu.VMEM((27, RADIAL, 2, 8, LANES), jnp.float32),
@@ -531,11 +543,13 @@
             pltpu.VMEM((27, RADIAL, FRAME, LANES), jnp.float32),
             pltpu.VMEM((27, 8, LANES), jnp.float32),
             pltpu.VMEM(block, jnp.float32),
+            pltpu.SMEM((1, COUNT), jnp.int32),
             pltpu.SemaphoreType.DMA((9,)),
+            pltpu.SemaphoreType.DMA(()),
         ],
         compiler_params=params,
         name="finish",
-    )(tile_offsets, relax_rates, post, strips, slots, below, above)
+    )(tile_offsets, scales, post, strips, slots, below, above)
     return out[None]
 
 

time: 46.2 us -> 45.5 us (0.985)
  Pallas kernels: 6.13 us -> 5.36 us
    pallas_call x1, Pallas kernels: 1.13 us -> 0.57 us  [local(): pl.pallas_call(edge_kernel, out_shape=(shape(block), shape((2 * COUNT, SL...]
where the time goes in v4:
time: 45.5 us; the launch traced here: 45.3 us
  blocking collectives  22.4 us (49%)
  starting transfers between devices  13.9 us (31%)
  Pallas kernels  5.36 us (12%)
  waiting for transfers between devices  2.58 us (6%)
  local copies, waits for them, and re-layouts  1.1 us (2%)
    all_to_all x1, blocking collectives, local(): lax.all_to_all(slots, ('grp', 'az'), split_axis=0, concat_axis=0, tiled=T...  22.4 us
    ppermute x1, starting transfers between devices, local(): above = lax.ppermute(message, 'ax', [(j, i) for i, j in up])  11.9 us
    pallas_call x1, Pallas kernels, local(): pl.pallas_call(finish_kernel, out_shape=shape(block), in_specs=[hbm] + [v...  3.12 us
    ppermute x1, waiting for transfers between devices, local(): below = lax.ppermute(message, 'ax', up)  2.58 us
    ppermute x1, starting transfers between devices, local(): below = lax.ppermute(message, 'ax', up)  1.92 us
    pallas_call x1, Pallas kernels, local(): pl.pallas_call(collide_kernel, out_shape=(shape(block), shape((2 * COUNT,...  1.29 us
    unnamed x6, local copies, waits for them, and re-layouts  1.1 us
  transfers between devices with their start and end apart: 2, of which 1 were waited for; matrix products, arithmetic and copies ran while one was open for 0% of the time, Pallas kernels for 3%

profile of v4, /device:TPU:1, one launch (start us, length us, event | category | flops | bytes accessed | tf_op | source)
XLA Modules:
  0.0 45.3 jit_solution(5201756858502765062)
XLA Ops:
  0.0 0.0 copy-start
  0.0 0.0 copy-start.1
  0.0 0.7 %copy-done.1 = s32[1,16]{1,0:T(1,128)S(1)} copy-done((s32[1,16]{1,0:T(1,128)S(1)}, s32[1,16]{1,0:T(1,128)}, u32[]{:S(2)}) %copy-start.1) | copy-done | bytes 88
  0.7 0.1 number.1.columns
  0.8 0.4 copy-done
  1.2 0.0 copy-start.2
  1.2 0.3 pack.1
  1.5 11.9 %collective-permute-start.1 = (f32[7,8,128]{2,1,0:T(8,128)S(1)}, f32[7,8,128]{2,1,0:T(8,128)S(1)}, u32[]{:S(2)}, u32[]{:S(2)}) collective-permute-start(f32[7,8,128]{2,1,0:T(8,128)S(1)} %pack.1), channel_id=1, source_target_pairs={{1,0},{2,1},{3,2},{4,3},{5,4},{6,5},{7,6},{8,7},{9,8},{10,9},{11,1... | collective-permute-start | bytes 86024 | tf_op jit(solution)/shard_map/ppermute | solution.py:512
  13.4 1.9 %collective-permute-start = (f32[7,8,128]{2,1,0:T(8,128)S(1)}, f32[7,8,128]{2,1,0:T(8,128)S(1)}, u32[]{:S(2)}, u32[]{:S(2)}) collective-permute-start(f32[7,8,128]{2,1,0:T(8,128)S(1)} %pack.1), channel_id=1, source_target_pairs={{0,1},{1,2},{2,3},{3,4},{4,5},{5,6},{6,7},{7,8},{8,9},{9,10},{10,1... | collective-permute-start | bytes 86024 | tf_op jit(solution)/shard_map/ppermute | solution.py:511
  15.4 0.0 copy-done.2
  15.4 1.3 %collide.1 = (f32[27,2,32,128]{3,2,1,0:T(8,128)S(1)}, f32[32,40,128]{2,1,0:T(8,128)S(1)}, f32[28,8,128]{2,1,0:T(8,128)S(1)}) custom-call(s32[1,16]{1,0:T(1,128)S(1)} %copy-done.1, f32[2,27]{1,0:T(2,128)S(1)} %copy-done.2, f32[27,2,32,128]{3,2,1,0:T(8,128)S(1)} %bitcast.3), custom_call_target="tpu_custom_call" | custom-call | flops 80000000 | bytes 1800000 | tf_op jit(solution)/shard_map/collide/pallas_call | solution.py:513
  16.7 0.0 collective-permute-done.1.above
  16.7 2.6 %collective-permute-done.below = f32[7,8,128]{2,1,0:T(8,128)S(1)} collective-permute-done((f32[7,8,128]{2,1,0:T(8,128)S(1)}, f32[7,8,128]{2,1,0:T(8,128)S(1)}, u32[]{:S(2)}, u32[]{:S(2)}) %collective-permute-start) | collective-permute-done | bytes 28704 | tf_op jit(solution)/shard_map/ppermute | solution.py:511
  19.3 0.6 %edge.1 = (f32[27,2,32,128]{3,2,1,0:T(8,128)S(1)}, f32[32,40,128]{2,1,0:T(8,128)S(1)}) custom-call(f32[28,8,128]{2,1,0:T(8,128)S(1)} %get-tuple-element.10.scales, f32[27,2,32,128]{3,2,1,0:T(8,128)S(1)} %get-tuple-element.11.post, f32[7,8,128]{2,1,0:T(8,128)S(1)} %collective-permute-done.below, f32[7,8,128]{2,1,0:T(8,128)S(1)} %collective-permute-done.1.above, ...), custom_call_target="tpu_custom_call" | custom-call | tf_op jit(solution)/shard_map/edge/pallas_call | solution.py:523
  19.8 22.4 %all_to_all.5.slots = f32[32,40,128]{2,1,0:T(8,128)S(1)} all-to-all(f32[32,40,128]{2,1,0:T(8,128)S(1)} %get-tuple-element.14), channel_id=1, replica_groups=mesh['grp'=2,'az'=16,'ax'=16] {'grp','az'}, dimensions={0} | all-to-all | bytes 1310720 | tf_op jit(solution)/shard_map/all_to_all | solution.py:532
  42.2 3.1 %finish.1 = f32[27,2,32,128]{3,2,1,0:T(8,128)} custom-call(s32[1,16]{1,0:T(1,128)S(1)} %copy-done.1, f32[28,8,128]{2,1,0:T(8,128)S(1)} %get-tuple-element.10.scales, f32[27,2,32,128]{3,2,1,0:T(8,128)S(1)} %get-tuple-element.11.post, f32[27,2,32,128]{3,2,1,0:T(8,128)S(1)} %get-tuple-element.13.strips, f32[32,40,128]{2,1,0:T(8,128)S(1)} %all_to_all.5.slots, ...), custom_call_target="tpu_custom_call" | custom-call | tf_op jit(solution)/shard_map/finish/pallas_call | solution.py:533
Async XLA Ops:
  0.0 1.2 %copy-start = (f32[1,27,2,32,128]{4,3,2,1,0:T(8,128)S(1)}, f32[1,27,2,32,128]{4,3,2,1,0:T(8,128)}, u32[]{:S(2)}) copy-start(f32[1,27,2,32,128]{4,3,2,1,0:T(8,128)} %param.3) | copy-start | bytes 2654212
  0.0 0.7 %copy-start.1 = (s32[1,16]{1,0:T(1,128)S(1)}, s32[1,16]{1,0:T(1,128)}, u32[]{:S(2)}) copy-start(s32[1,16]{1,0:T(1,128)} %numbers.1) | copy-start | bytes 196
  1.2 14.2 %copy-start.2 = (f32[2,27]{1,0:T(2,128)S(1)}, f32[2,27]{1,0:T(2,128)}, u32[]{:S(2)}) copy-start(f32[2,27]{1,0:T(2,128)} %rates.1) | copy-start | bytes 652
  1.5 15.2 %collective-permute-start.1 = (f32[7,8,128]{2,1,0:T(8,128)S(1)}, f32[7,8,128]{2,1,0:T(8,128)S(1)}, u32[]{:S(2)}, u32[]{:S(2)}) collective-permute-start(f32[7,8,128]{2,1,0:T(8,128)S(1)} %pack.1), channel_id=1, source_target_pairs={{1,0},{2,1},{3,2},{4,3},{5,4},{6,5},{7,6},{8,7},{9,8},{10,9},{11,1... | collective-permute-start | bytes 86024 | tf_op jit(solution)/shard_map/ppermute | solution.py:512
  13.4 5.8 %collective-permute-start = (f32[7,8,128]{2,1,0:T(8,128)S(1)}, f32[7,8,128]{2,1,0:T(8,128)S(1)}, u32[]{:S(2)}, u32[]{:S(2)}) collective-permute-start(f32[7,8,128]{2,1,0:T(8,128)S(1)} %pack.1), channel_id=1, source_target_pairs={{0,1},{1,2},{2,3},{3,4},{4,5},{5,6},{6,7},{7,8},{8,9},{9,10},{10,1... | collective-permute-start | bytes 86024 | tf_op jit(solution)/shard_map/ppermute | solution.py:511

commit v5 on v4

--- a/solution.py
+++ b/solution.py
@@ -77,11 +77,6 @@
     return [g[i] - d[i] for i in range(27)]
 
 
-def face_factor(rates, group):
-    fine, coarse = rates[0, 12], rates[1, 12]
-    return jnp.where(group == 0, 2.0 * fine / coarse, coarse / (2.0 * fine))
-
-
 def rescaled(before, after, group, factor):
     m = moments(before)
     rho = m[0] * (1.0 / 216.0)
@@ -181,18 +176,22 @@
             message[i // 4] = acc
 
 
-def collide_kernel(offsets, rates, pops, post, slots, scales, face):
+def collide_kernel(numbers, rates, pops, post, slots, scales, face, offsets, small):
+    fetch = pltpu.make_async_copy(numbers, offsets, small)
+    fetch.start()
     group, place = group_and_place()
     own, other = COUNT * group, COUNT * (1 - group)
-    factor = face_factor(rates, group)
-    scaled = [rates[group, k] * 0.125 for k in range(27)]
-    for k, value in enumerate(scaled + [factor]):
-        scales[k] = jnp.full((8, LANES), value, jnp.float32)
+    mine = jnp.where(group == 0, rates[0:1, :], rates[1:2, :])
+    for k in range(27):
+        scales[k] = jnp.broadcast_to(mine[:, k : k + 1] * 0.125, (8, LANES))
+    fine, coarse = rates[0:1, 12:13], rates[1:2, 12:13]
+    factor = jnp.broadcast_to(jnp.where(group == 0, 2.0 * fine / coarse, coarse / (2.0 * fine)), (8, LANES))
+    scales[27] = factor
 
     def chunk(step, carry):
         r, rows = step // 4, pl.ds(pl.multiple_of(step % 4 * 8, 8), 8)
         g = [pops[i, r, rows, :] for i in range(27)]
-        for i, value in enumerate(relax(g, scaled)):
+        for i, value in enumerate(relax(g, [scales[k] for k in range(27)])):
             post[i, r, rows, :] = value
         return carry
 
@@ -219,6 +218,7 @@
     def _():
         halos(False)
 
+    fetch.wait()
     for q in range(COUNT):
         slot = other + partner(place, group, offsets[0, q])
         for i in range(9):
@@ -488,7 +488,7 @@
     shape = functools.partial(jax.ShapeDtypeStruct, dtype=jnp.float32)
     block = (27, RADIAL, ROWS, LANES)
     params = pltpu.CompilerParams(vmem_limit_bytes=24 << 20)
-    smem, vmem, hbm = [pl.BlockSpec(memory_space=m) for m in (pltpu.SMEM, pltpu.VMEM, pltpu.HBM)]
+    vmem, hbm = [pl.BlockSpec(memory_space=m) for m in (pltpu.VMEM, pltpu.HBM)]
     columns = pl.pallas_call(
         number_kernel,
         out_shape=shape((8, LANES)),
@@ -513,9 +513,13 @@
     post, slots, scales = pl.pallas_call(
         collide_kernel,
         out_shape=(shape(block), shape((2 * COUNT, SLOT_ROWS, LANES)), shape((28, 8, LANES))),
-        in_specs=[smem, smem, vmem],
+        in_specs=[hbm, vmem, vmem],
         out_specs=(vmem, vmem, vmem),
-        scratch_shapes=[pltpu.VMEM((9, ROWS, LANES), jnp.float32)],
+        scratch_shapes=[
+            pltpu.VMEM((9, ROWS, LANES), jnp.float32),
+            pltpu.SMEM((1, COUNT), jnp.int32),
+            pltpu.SemaphoreType.DMA(()),
+        ],
         compiler_params=params,
         cost_estimate=pl.CostEstimate(flops=80_000_000, bytes_accessed=1_800_000, transcendentals=0),
         name="collide",

time: 45.5 us -> 45.5 us (level)
  transfers between devices with their start and end apart: 2 -> 2, of which waited for: 1 -> 1; matrix products, arithmetic and copies ran while one was open for 0% -> 0% of each run, Pallas kernels for 3% -> 2%
where the time goes in v5:
time: 45.5 us; the launch traced here: 45.3 us
  blocking collectives  22.4 us (49%)
  starting transfers between devices  13.9 us (31%)
  Pallas kernels  4.94 us (11%)
  waiting for transfers between devices  3 us (7%)
  local copies, waits for them, and re-layouts  1.1 us (2%)
    all_to_all x1, blocking collectives, local(): lax.all_to_all(slots, ('grp', 'az'), split_axis=0, concat_axis=0, tiled=T...  22.4 us
    ppermute x1, starting transfers between devices, local(): above = lax.ppermute(message, 'ax', [(j, i) for i, j in up])  11.9 us
    pallas_call x1, Pallas kernels, local(): pl.pallas_call(finish_kernel, out_shape=shape(block), in_specs=[hbm] + [v...  3.12 us
    ppermute x1, waiting for transfers between devices, local(): below = lax.ppermute(message, 'ax', up)  3 us
    ppermute x1, starting transfers between devices, local(): below = lax.ppermute(message, 'ax', up)  1.92 us
    unnamed x6, local copies, waits for them, and re-layouts  1.1 us
  transfers between devices with their start and end apart: 2, of which 1 were waited for; matrix products, arithmetic and copies ran while one was open for 0% of the time, Pallas kernels for 2%

profile of v5, /device:TPU:1, one launch (start us, length us, event | category | flops | bytes accessed | tf_op | source)
XLA Modules:
  0.0 45.3 jit_solution(5044162522711407090)
XLA Ops:
  0.0 0.0 copy-start
  0.0 0.0 copy-start.1
  0.0 0.7 %copy-done.1 = s32[1,16]{1,0:T(1,128)S(1)} copy-done((s32[1,16]{1,0:T(1,128)S(1)}, s32[1,16]{1,0:T(1,128)}, u32[]{:S(2)}) %copy-start.1) | copy-done | bytes 88
  0.7 0.1 number.1.columns
  0.8 0.4 copy-done
  1.2 0.0 copy-start.2
  1.2 0.3 pack.1
  1.5 11.9 %collective-permute-start.1 = (f32[7,8,128]{2,1,0:T(8,128)S(1)}, f32[7,8,128]{2,1,0:T(8,128)S(1)}, u32[]{:S(2)}, u32[]{:S(2)}) collective-permute-start(f32[7,8,128]{2,1,0:T(8,128)S(1)} %pack.1), channel_id=1, source_target_pairs={{1,0},{2,1},{3,2},{4,3},{5,4},{6,5},{7,6},{8,7},{9,8},{10,9},{11,1... | collective-permute-start | bytes 86024 | tf_op jit(solution)/shard_map/ppermute | solution.py:512
  13.4 1.9 %collective-permute-start = (f32[7,8,128]{2,1,0:T(8,128)S(1)}, f32[7,8,128]{2,1,0:T(8,128)S(1)}, u32[]{:S(2)}, u32[]{:S(2)}) collective-permute-start(f32[7,8,128]{2,1,0:T(8,128)S(1)} %pack.1), channel_id=1, source_target_pairs={{0,1},{1,2},{2,3},{3,4},{4,5},{5,6},{6,7},{7,8},{8,9},{9,10},{10,1... | collective-permute-start | bytes 86024 | tf_op jit(solution)/shard_map/ppermute | solution.py:511
  15.4 0.0 copy-done.2
  15.4 0.9 %collide.1 = (f32[27,2,32,128]{3,2,1,0:T(8,128)S(1)}, f32[32,40,128]{2,1,0:T(8,128)S(1)}, f32[28,8,128]{2,1,0:T(8,128)S(1)}) custom-call(s32[1,16]{1,0:T(1,128)S(1)} %copy-done.1, f32[2,27]{1,0:T(2,128)S(1)} %copy-done.2, f32[27,2,32,128]{3,2,1,0:T(8,128)S(1)} %bitcast.3), custom_call_target="tpu_custom_call" | custom-call | flops 80000000 | bytes 1800000 | tf_op jit(solution)/shard_map/collide/pallas_call | solution.py:513
  16.2 0.0 collective-permute-done.1.above
  16.3 3.0 %collective-permute-done.below = f32[7,8,128]{2,1,0:T(8,128)S(1)} collective-permute-done((f32[7,8,128]{2,1,0:T(8,128)S(1)}, f32[7,8,128]{2,1,0:T(8,128)S(1)}, u32[]{:S(2)}, u32[]{:S(2)}) %collective-permute-start) | collective-permute-done | bytes 28704 | tf_op jit(solution)/shard_map/ppermute | solution.py:511
  19.3 0.6 %edge.1 = (f32[27,2,32,128]{3,2,1,0:T(8,128)S(1)}, f32[32,40,128]{2,1,0:T(8,128)S(1)}) custom-call(f32[28,8,128]{2,1,0:T(8,128)S(1)} %get-tuple-element.10.scales, f32[27,2,32,128]{3,2,1,0:T(8,128)S(1)} %get-tuple-element.11.post, f32[7,8,128]{2,1,0:T(8,128)S(1)} %collective-permute-done.below, f32[7,8,128]{2,1,0:T(8,128)S(1)} %collective-permute-done.1.above, ...), custom_call_target="tpu_custom_call" | custom-call | tf_op jit(solution)/shard_map/edge/pallas_call | solution.py:527
  19.8 22.4 %all_to_all.5.slots = f32[32,40,128]{2,1,0:T(8,128)S(1)} all-to-all(f32[32,40,128]{2,1,0:T(8,128)S(1)} %get-tuple-element.14), channel_id=1, replica_groups=mesh['grp'=2,'az'=16,'ax'=16] {'grp','az'}, dimensions={0} | all-to-all | bytes 1310720 | tf_op jit(solution)/shard_map/all_to_all | solution.py:536
  42.2 3.1 %finish.1 = f32[27,2,32,128]{3,2,1,0:T(8,128)} custom-call(s32[1,16]{1,0:T(1,128)S(1)} %copy-done.1, f32[28,8,128]{2,1,0:T(8,128)S(1)} %get-tuple-element.10.scales, f32[27,2,32,128]{3,2,1,0:T(8,128)S(1)} %get-tuple-element.11.post, f32[27,2,32,128]{3,2,1,0:T(8,128)S(1)} %get-tuple-element.13.strips, f32[32,40,128]{2,1,0:T(8,128)S(1)} %all_to_all.5.slots, ...), custom_call_target="tpu_custom_call" | custom-call | tf_op jit(solution)/shard_map/finish/pallas_call | solution.py:537
Async XLA Ops:
  0.0 1.2 %copy-start = (f32[1,27,2,32,128]{4,3,2,1,0:T(8,128)S(1)}, f32[1,27,2,32,128]{4,3,2,1,0:T(8,128)}, u32[]{:S(2)}) copy-start(f32[1,27,2,32,128]{4,3,2,1,0:T(8,128)} %param.3) | copy-start | bytes 2654212
  0.0 0.7 %copy-start.1 = (s32[1,16]{1,0:T(1,128)S(1)}, s32[1,16]{1,0:T(1,128)}, u32[]{:S(2)}) copy-start(s32[1,16]{1,0:T(1,128)} %numbers.3) | copy-start | bytes 196
  1.2 14.2 %copy-start.2 = (f32[2,27]{1,0:T(2,128)S(1)}, f32[2,27]{1,0:T(2,128)}, u32[]{:S(2)}) copy-start(f32[2,27]{1,0:T(2,128)} %rates.1) | copy-start | bytes 652
  1.5 14.8 %collective-permute-start.1 = (f32[7,8,128]{2,1,0:T(8,128)S(1)}, f32[7,8,128]{2,1,0:T(8,128)S(1)}, u32[]{:S(2)}, u32[]{:S(2)}) collective-permute-start(f32[7,8,128]{2,1,0:T(8,128)S(1)} %pack.1), channel_id=1, source_target_pairs={{1,0},{2,1},{3,2},{4,3},{5,4},{6,5},{7,6},{8,7},{9,8},{10,9},{11,1... | collective-permute-start | bytes 86024 | tf_op jit(solution)/shard_map/ppermute | solution.py:512
  13.4 5.8 %collective-permute-start = (f32[7,8,128]{2,1,0:T(8,128)S(1)}, f32[7,8,128]{2,1,0:T(8,128)S(1)}, u32[]{:S(2)}, u32[]{:S(2)}) collective-permute-start(f32[7,8,128]{2,1,0:T(8,128)S(1)} %pack.1), channel_id=1, source_target_pairs={{0,1},{1,2},{2,3},{3,4},{4,5},{5,6},{6,7},{7,8},{8,9},{9,10},{10,1... | collective-permute-start | bytes 86024 | tf_op jit(solution)/shard_map/ppermute | solution.py:511
